TPU v7x, 32 devices: a whole 2x2x4 slice. The times are simulated.
32 devices in a mesh: dp: 4 (over x, core), ctx: 4 (over z), tensor: 2 (over y).
Axes of the slice: x: 2, y: 2, z: 4, core: 2. Of those that a mesh axis runs over, the one named last changes fastest.
Arguments:
- tokens: bfloat16 [4, 1024, 1024], P('dp', 'ctx'), may hold values from -6 to 6
- seq_lengths: int32 [4], P('dp'), may hold values from 256 to 1024, as said below
- qkv_weight: bfloat16 [1024, 3, 1024], P(('dp', 'ctx'), None, 'tensor'), may hold values from -4 to 4
- out_weight: bfloat16 [1024, 1024], P(('dp', 'ctx'), 'tensor'), may hold values from -1.5 to 1.5
- up_weight: bfloat16 [1024, 4096], P(('dp', 'ctx'), 'tensor'), may hold values from -0.1875 to 0.1875
- down_weight: bfloat16 [1024, 4096], P(('dp', 'ctx'), 'tensor'), may hold values from -0.09375 to 0.09375
- head_bias: bfloat16 [16, 128], P('tensor', ('dp', 'ctx')), may hold values from -3 to 3
- hidden_bias: bfloat16 [32, 128], P('tensor', ('dp', 'ctx')), may hold values from -3 to 3
- norm_gains: bfloat16 [2, 1024], P(None, ('dp', 'ctx')), may hold values from 0.25 to 1.75
- out_biases: bfloat16 [4, 1024], P(None, ('dp', 'ctx')), may hold values from -3 to 3
- cotangent: bfloat16 [4, 1024, 1024], P('dp', 'ctx'), may hold values from -6 to 6
Outputs:
- output: bfloat16 [4, 1024, 1024], P('dp', 'ctx')
- input_grad: float32 [4, 1024, 1024], P('dp', 'ctx')
- qkv_grad: float32 [1024, 3, 1024], P(('dp', 'ctx'), None, 'tensor')
- out_weight_grad: float32 [1024, 1024], P(('dp', 'ctx'), 'tensor')
- up_grad: float32 [1024, 4096], P(('dp', 'ctx'), 'tensor')
- down_grad: float32 [1024, 4096], P(('dp', 'ctx'), 'tensor')
- head_bias_grad: float32 [16, 128], P('tensor', ('dp', 'ctx'))
- hidden_bias_grad: float32 [32, 128], P('tensor', ('dp', 'ctx'))
- gains_grad: float32 [2, 1024], P(None, ('dp', 'ctx'))
- biases_grad: float32 [4, 1024], P(None, ('dp', 'ctx'))
Inputs may be any that keep to these rules, and one draw needn't show every extreme that they name: `seq_lengths`: valid tokens of each sequence; in every draw some sequence has exactly 1024.
All inputs are finite; a program needn't handle non-finite values.
Results may differ from a plain program's by a relative error of at most 0.011.
The roundings to bfloat16 on the way count: a program that leaves them out, or rounds other values in their place, can miss the bound.
Values may be sent and summed in bfloat16 or wider, within the bound.
A program may use at most 128 MiB of HBM per device.

v0:
```python
import math

import jax
import jax.numpy as jnp
from jax import lax
from jax.sharding import PartitionSpec as P

EPSILON = 1e-05
SCALE = 0.125
NEG_BIG = -1000000000.0
INV_ROOT_TWO = 1.0 / math.sqrt(2.0)
INV_ROOT_TWO_PI = 1.0 / math.sqrt(2.0 * math.pi)


def contract_last(left, right):
    return lax.dot_general(
        left, right, (((1,), (1,)), ((), ())), preferred_element_type=jnp.float32
    )


def contract_first(left, right):
    return lax.dot_general(
        left, right, (((0,), (0,)), ((), ())), preferred_element_type=jnp.float32
    )


def layer_norm(hidden_in, gain, shift):
    centred = hidden_in - jnp.mean(hidden_in, axis=-1, keepdims=True)
    variance = jnp.mean(centred * centred, axis=-1, keepdims=True)
    inv_std = lax.rsqrt(variance + EPSILON)
    normed = centred * inv_std
    return (normed * gain + shift, normed, inv_std)


def norm_back(grad_out, normed, inv_std, gain):
    grad_normed = grad_out * gain
    first_mean = jnp.mean(grad_normed, axis=-1, keepdims=True)
    second_mean = jnp.mean(grad_normed * normed, axis=-1, keepdims=True)
    grad_in = inv_std * (grad_normed - first_mean - normed * second_mean)
    return (grad_in, jnp.sum(grad_out * normed, axis=0), jnp.sum(grad_out, axis=0))


def gelu_parts(pre_act):
    cdf_val = 0.5 * (1.0 + jax.scipy.special.erf(pre_act * INV_ROOT_TWO))
    return (
        pre_act * cdf_val,
        cdf_val + pre_act * jnp.exp(-0.5 * pre_act * pre_act) * INV_ROOT_TWO_PI,
    )


def block_scores(queries, key_rows, valid):
    scores = (
        jnp.einsum("qhd,khd->hqk", queries, key_rows, preferred_element_type=jnp.float32) * SCALE
    )
    return jnp.where(valid[None, None, :], scores, NEG_BIG)


def attend_forward(inputs):
    queries, key_rows, value_rows, valid = inputs
    scores = block_scores(queries, key_rows, valid)
    peak = jnp.max(scores, axis=-1, keepdims=True)
    log_total = peak + jnp.log(jnp.sum(jnp.exp(scores - peak), axis=-1, keepdims=True))
    probs = jnp.exp(scores - log_total).astype(jnp.bfloat16)
    mixed = jnp.einsum(
        "hqk,khd->qhd", probs, value_rows, preferred_element_type=jnp.float32
    ).astype(jnp.bfloat16)
    return (mixed, log_total)


def attend_backward(inputs):
    queries, key_rows, value_rows, valid, mixed, log_total, grad_mixed = inputs
    scores = block_scores(queries, key_rows, valid)
    probs = jnp.exp(scores - log_total)
    grad_values = jnp.einsum(
        "hqk,qhd->khd", probs.astype(jnp.bfloat16), grad_mixed, preferred_element_type=jnp.float32
    )
    grad_probs = jnp.einsum(
        "qhd,khd->hqk", grad_mixed, value_rows, preferred_element_type=jnp.float32
    )
    inner = jnp.einsum("qhd,qhd->hq", grad_mixed.astype(jnp.float32), mixed.astype(jnp.float32))
    grad_scores = (probs * (grad_probs - inner[:, :, None])).astype(jnp.bfloat16)
    grad_queries = (
        jnp.einsum("hqk,khd->qhd", grad_scores, key_rows, preferred_element_type=jnp.float32)
        * SCALE
    )
    grad_keys = (
        jnp.einsum("hqk,qhd->khd", grad_scores, queries, preferred_element_type=jnp.float32) * SCALE
    )
    return (grad_queries, grad_keys, grad_values)


def on_device(
    tokens,
    seq_lengths,
    qkv_weight,
    out_weight,
    up_weight,
    down_weight,
    head_bias,
    hidden_bias,
    norm_gains,
    out_biases,
    cotangent,
):
    seq_count, local_len, width = tokens.shape
    row_count = seq_count * local_len
    gathered = (
        lax.all_gather(qkv_weight, ("dp", "ctx"), axis=0, tiled=True),
        lax.all_gather(out_weight, ("dp", "ctx"), axis=0, tiled=True),
        lax.all_gather(up_weight, ("dp", "ctx"), axis=0, tiled=True),
        lax.all_gather(down_weight, ("dp", "ctx"), axis=0, tiled=True),
        lax.all_gather(head_bias, ("dp", "ctx"), axis=1, tiled=True),
        lax.all_gather(hidden_bias, ("dp", "ctx"), axis=1, tiled=True),
        lax.all_gather(norm_gains, ("dp", "ctx"), axis=1, tiled=True),
        lax.all_gather(out_biases, ("dp", "ctx"), axis=1, tiled=True),
    )
    qkv_full, out_full, up_full, down_full, head_full, hidden_full, gains_full, biases_full = (
        gathered
    )
    local_width = qkv_full.shape[2]
    local_heads = head_full.shape[0]
    head_size = head_full.shape[1] // 2
    bias_query = head_full[:, :head_size].reshape(local_width).astype(jnp.float32)
    bias_value = head_full[:, head_size:].reshape(local_width).astype(jnp.float32)
    bias_hidden = hidden_full.reshape(-1).astype(jnp.float32)
    gains_wide = gains_full.astype(jnp.float32)
    biases_wide = biases_full.astype(jnp.float32)
    token_rows = tokens.reshape(row_count, width)
    projected = jnp.dot(
        token_rows, qkv_full.reshape(width, 3 * local_width), preferred_element_type=jnp.float32
    ).reshape(row_count, 3, local_width)
    head_shape = (seq_count, local_len, local_heads, head_size)
    queries = (projected[:, 0] + bias_query).astype(jnp.bfloat16).reshape(head_shape)
    key_local = projected[:, 1].astype(jnp.bfloat16).reshape(head_shape)
    value_local = (projected[:, 2] + bias_value).astype(jnp.bfloat16).reshape(head_shape)
    key_rows, value_rows = (
        lax.all_gather(key_local, "ctx", axis=1, tiled=True),
        lax.all_gather(value_local, "ctx", axis=1, tiled=True),
    )
    total_len = key_rows.shape[1]
    valid = jnp.arange(total_len)[None, :] < seq_lengths[:, None]
    mixed, log_total = lax.map(attend_forward, (queries, key_rows, value_rows, valid))
    attn_flat = mixed.reshape(row_count, local_width)
    attn_proj = lax.psum(contract_last(attn_flat, out_full), "tensor")
    first_sum = token_rows.astype(jnp.float32) + attn_proj + biases_wide[0]
    normed_one, z_one, rstd_one = layer_norm(first_sum, gains_wide[0], biases_wide[1])
    normed_low = normed_one.astype(jnp.bfloat16)
    pre_act = jnp.dot(normed_low, up_full, preferred_element_type=jnp.float32) + bias_hidden
    activated, slope = gelu_parts(pre_act)
    hidden_low = activated.astype(jnp.bfloat16)
    mlp_out = lax.psum(contract_last(hidden_low, down_full), "tensor")
    second_sum = normed_one + mlp_out + biases_wide[2]
    result, z_two, rstd_two = layer_norm(second_sum, gains_wide[1], biases_wide[3])
    output = result.astype(jnp.bfloat16).reshape(seq_count, local_len, width)
    qkv_back, out_back, up_back, down_back = (qkv_full, out_full, up_full, down_full)
    grad_out = cotangent.reshape(row_count, width).astype(jnp.float32)
    grad_two, gain_two_grad, shift_two_grad = norm_back(grad_out, z_two, rstd_two, gains_wide[1])
    grad_two_low = grad_two.astype(jnp.bfloat16)
    down_part = contract_first(grad_two_low, hidden_low)
    grad_hidden = jnp.dot(grad_two_low, down_back, preferred_element_type=jnp.float32)
    grad_pre = grad_hidden * slope
    grad_pre_low = grad_pre.astype(jnp.bfloat16)
    up_part = contract_first(normed_low, grad_pre_low)
    hidden_part = jnp.sum(grad_pre, axis=0).reshape(hidden_full.shape)
    grad_normed = lax.psum(contract_last(grad_pre_low, up_back), "tensor") + grad_two
    grad_one, gain_one_grad, shift_one_grad = norm_back(grad_normed, z_one, rstd_one, gains_wide[0])
    grad_one_low = grad_one.astype(jnp.bfloat16)
    out_part = contract_first(grad_one_low, attn_flat)
    grad_attn = (
        jnp.dot(grad_one_low, out_back, preferred_element_type=jnp.float32)
        .astype(jnp.bfloat16)
        .reshape(head_shape)
    )
    grad_queries, key_terms, value_terms = lax.map(
        attend_backward, (queries, key_rows, value_rows, valid, mixed, log_total, grad_attn)
    )
    grad_keys, grad_values = (
        lax.psum_scatter(key_terms, "ctx", scatter_dimension=1, tiled=True),
        lax.psum_scatter(value_terms, "ctx", scatter_dimension=1, tiled=True),
    )
    query_flat = grad_queries.reshape(row_count, local_width)
    value_flat = grad_values.reshape(row_count, local_width)
    grad_proj = (
        jnp.stack([query_flat, grad_keys.reshape(row_count, local_width), value_flat], axis=1)
        .astype(jnp.bfloat16)
        .reshape(row_count, 3 * local_width)
    )
    qkv_part = contract_first(token_rows, grad_proj).reshape(width, 3, local_width)
    input_part = contract_last(grad_proj, qkv_back.reshape(width, 3 * local_width))
    input_grad = (lax.psum(input_part, "tensor") + grad_one).reshape(seq_count, local_len, width)
    head_part = jnp.concatenate(
        [
            jnp.sum(query_flat, axis=0).reshape(local_heads, head_size),
            jnp.sum(value_flat, axis=0).reshape(local_heads, head_size),
        ],
        axis=1,
    )
    gains_part = jnp.stack([gain_one_grad, gain_two_grad])
    biases_part = jnp.stack(
        [jnp.sum(grad_one, axis=0), shift_one_grad, jnp.sum(grad_two, axis=0), shift_two_grad]
    )
    summed = (
        lax.psum_scatter(qkv_part, ("dp", "ctx"), scatter_dimension=0, tiled=True),
        lax.psum_scatter(out_part, ("dp", "ctx"), scatter_dimension=0, tiled=True),
        lax.psum_scatter(up_part, ("dp", "ctx"), scatter_dimension=0, tiled=True),
        lax.psum_scatter(down_part, ("dp", "ctx"), scatter_dimension=0, tiled=True),
        lax.psum_scatter(head_part, ("dp", "ctx"), scatter_dimension=1, tiled=True),
        lax.psum_scatter(hidden_part, ("dp", "ctx"), scatter_dimension=1, tiled=True),
        lax.psum_scatter(gains_part, ("dp", "ctx"), scatter_dimension=1, tiled=True),
        lax.psum_scatter(biases_part, ("dp", "ctx"), scatter_dimension=1, tiled=True),
    )
    return (
        output,
        input_grad,
        summed[0],
        summed[1],
        summed[2],
        summed[3],
        summed[4],
        summed[5],
        summed[6],
        summed[7],
    )


def solution(mesh):
    in_specs = (
        P("dp", "ctx", None),
        P("dp"),
        P(("dp", "ctx"), None, "tensor"),
        P(("dp", "ctx"), "tensor"),
        P(("dp", "ctx"), "tensor"),
        P(("dp", "ctx"), "tensor"),
        P("tensor", ("dp", "ctx")),
        P("tensor", ("dp", "ctx")),
        P(None, ("dp", "ctx")),
        P(None, ("dp", "ctx")),
        P("dp", "ctx", None),
    )
    out_specs = (
        P("dp", "ctx", None),
        P("dp", "ctx", None),
        P(("dp", "ctx"), None, "tensor"),
        P(("dp", "ctx"), "tensor"),
        P(("dp", "ctx"), "tensor"),
        P(("dp", "ctx"), "tensor"),
        P("tensor", ("dp", "ctx")),
        P("tensor", ("dp", "ctx")),
        P(None, ("dp", "ctx")),
        P(None, ("dp", "ctx")),
    )
    return jax.shard_map(
        on_device, mesh=mesh, in_specs=in_specs, out_specs=out_specs, check_vma=False
    )
```

profile of v0, /device:TPU:0, one launch (start us, length us, event | category | flops | bytes accessed | tf_op | source)
XLA Modules:
  0.0 1045.7 jit_solution(3260139131030527384)
XLA Ops:
  8.0 50.5 %all-gather.9.cloned.1.call-done = bf16[1024,3,512]{2,0,1:T(8,128)(2,1)} async-done(((bf16[64,3,512]{2,0,1:T(8,128)(2,1)}), bf16[1024,3,512]{2,0,1:T(8,128)(2,1)}) %all-gather.9.cloned.1.call-update) | async-done | bytes 3145744 | tf_op jit(solution)/shard_map/all_gather | solution.py:108
  58.4 3.2 copy.61
  61.6 2.1 fusion.2
  65.9 30.8 %all_gather.31 = bf16[8,128]{0,1:T(8,128)(2,1)S(1)} all-gather(bf16[8,8]{0,1:T(8,128)(2,1)S(1)} %copy.63), channel_id=1, replica_groups=mesh['dp'=4,'ctx'=4,'tensor'=2] {'dp','ctx'}, dimensions={1}, use_global_device_ids=true | all-gather | bytes 2176 | tf_op jit(solution)/shard_map/all_gather | solution.py:112
  100.8 2.9 fusion.1
  103.7 2.0 exponential_reduce_fusion
  107.0 20.4 %all-gather.11.cloned.1.call-done = bf16[1,1024,8,64]{1,3,2,0:T(8,128)(2,1)} async-done(((bf16[1,256,8,64]{1,3,2,0:T(8,128)(2,1)}), bf16[1,1024,8,64]{1,3,2,0:T(8,128)(2,1)}) %all-gather.11.cloned.1.call-update) | async-done | bytes 1048592 | tf_op jit(solution)/shard_map/all_gather | solution.py:138
  127.4 5.6 convolution_convert_fusion.1
  132.9 32.7 %all-gather.15.cloned.1.call-done = bf16[1024,512]{1,0:T(8,128)(2,1)} async-done(((bf16[64,512]{1,0:T(8,128)(2,1)}), bf16[1024,512]{1,0:T(8,128)(2,1)}) %all-gather.15.cloned.1.call-update) | async-done | bytes 1048592 | tf_op jit(solution)/shard_map/all_gather | solution.py:109
  165.6 2.7 fusion.60
  169.7 30.6 %all-gather = bf16[16,64,4]{1,2,0:T(4,128)(2,1)S(1)} all-gather(bf16[1,64,4]{1,2,0:T(4,128)(2,1)S(1)} %bitcast.182), channel_id=1, replica_groups=mesh['dp'=4,'ctx'=4,'tensor'=2] {'dp','ctx'}, dimensions={0}, use_global_device_ids=true | all-gather | bytes 8704 | tf_op jit(solution)/shard_map/all_gather | solution.py:115
  200.4 28.8 %all-gather.1 = bf16[16,64,2]{1,2,0:T(2,128)(2,1)S(1)} all-gather(bf16[1,64,2]{1,2,0:T(2,128)(2,1)S(1)} %bitcast.183), channel_id=1, replica_groups=mesh['dp'=4,'ctx'=4,'tensor'=2] {'dp','ctx'}, dimensions={0}, use_global_device_ids=true | all-gather | bytes 4352 | tf_op jit(solution)/shard_map/all_gather | solution.py:114
  229.3 31.7 %all_gather.38 = bf16[16,128]{0,1:T(8,128)(2,1)S(1)} all-gather(bf16[16,8]{0,1:T(8,128)(2,1)S(1)} %copy-done.16), channel_id=1, replica_groups=mesh['dp'=4,'ctx'=4,'tensor'=2] {'dp','ctx'}, dimensions={1}, use_global_device_ids=true | all-gather | bytes 4352 | tf_op jit(solution)/shard_map/all_gather | solution.py:113
  261.2 1.4 fusion.52
  262.9 3.5 convolution_add_fusion
  266.5 45.1 %all-gather.19.cloned.1.call-done = bf16[1024,2048]{1,0:T(8,128)(2,1)} async-done(((bf16[64,2048]{1,0:T(8,128)(2,1)}), bf16[1024,2048]{1,0:T(8,128)(2,1)}) %all-gather.19.cloned.1.call-update) | async-done | bytes 4194320 | tf_op jit(solution)/shard_map/all_gather | solution.py:111
  311.6 4.4 fusion.47
  316.3 38.6 %all-reduce.10.cloned.1.call-done = f32[256,1024]{1,0:T(8,128)} async-done(((f32[256,1024]{1,0:T(8,128)}), f32[256,1024]{1,0:T(8,128)}) %all-reduce.10.cloned.1.call-update) | async-done | bytes 1048592 | tf_op jit(solution)/shard_map/psum | solution.py:151
  354.9 1.8 fusion.51
  357.5 2.3 fusion.49
  359.8 2.0 fusion.59
  362.0 2.3 fusion.31
  364.3 40.2 %all-reduce.12.cloned.1.call-done = f32[256,1024]{1,0:T(8,128)} async-done(((f32[256,1024]{1,0:T(8,128)}), f32[256,1024]{1,0:T(8,128)}) %all-reduce.12.cloned.1.call-update) | async-done | bytes 1048592 | tf_op jit(solution)/shard_map/psum | solution.py:165
  404.5 1.8 multiply_reduce_fusion
  406.6 2.4 convolution_convert_fusion
  411.2 5.6 multiply_convert_fusion
  416.7 2.0 copy-done.1
  418.7 2.2 multiply_bitcast_fusion
  421.0 6.6 convolution_bitcast_fusion
  429.9 4.0 fusion.54
  435.9 28.8 %reduce-scatter.15.cloned.1.call-done = f32[1,256,8,64]{1,3,2,0:T(8,128)} async-done(((f32[1,1024,8,64]{1,3,2,0:T(8,128)}), f32[1,256,8,64]{1,3,2,0:T(8,128)}) %reduce-scatter.15.cloned.1.call-update) | async-done | bytes 524304 | tf_op jit(solution)/shard_map/reduce_scatter | solution.py:178
  466.6 43.2 %reduce-scatter.17.cloned.1.call-done = f32[1,256,8,64]{1,3,2,0:T(8,128)} async-done(((f32[1,1024,8,64]{1,3,2,0:T(8,128)}), f32[1,256,8,64]{1,3,2,0:T(8,128)}) %reduce-scatter.17.cloned.1.call-update) | async-done | bytes 524304 | tf_op jit(solution)/shard_map/reduce_scatter | solution.py:179
  509.9 2.0 fusion.55
  511.9 1.8 copy.74
  513.7 4.1 convolution_bitcast_fusion.1
  518.1 1.8 fusion.33
  520.1 5.9 fusion.29
  526.0 6.2 fusion.36
  535.7 3.6 fusion.27
  539.3 6.5 copy.76
  547.7 21.0 %reduce-scatter.27.cloned.1.call-done = f32[64,2]{1,0:T(8,128)} async-done(((f32[1024,2]{1,0:T(8,128)}), f32[64,2]{1,0:T(8,128)}) %reduce-scatter.27.cloned.1.call-update) | async-done | bytes 528
  570.1 57.4 %reduce-scatter.29.cloned.1.call-done = f32[64,4]{1,0:T(8,128)} async-done(((f32[1024,4]{1,0:T(8,128)}), f32[64,4]{1,0:T(8,128)}) %reduce-scatter.29.cloned.1.call-update) | async-done | bytes 1040
  629.0 59.2 %all-reduce.2 = (f32[8,128]{1,0:T(8,128)S(1)}, f32[16,128]{1,0:T(8,128)S(1)}) all-reduce(f32[8,128]{1,0:T(8,128)S(1)} %pad_maximum_fusion.3, f32[16,128]{1,0:T(8,128)S(1)} %bitcast.181), channel_id=8, replica_groups=mesh['dp'=4,'ctx'=4,'tensor'=2] {'dp','ctx'}, use_global_device_ids=true, to_apply=%region_22.23.clone | all-reduce | flops 3072 | bytes 24576
  689.6 2.4 add_bitcast_fusion
  691.9 43.4 %reduce-scatter.21.cloned.1.call-done = f32[64,512]{1,0:T(8,128)} async-done(((f32[1024,512]{1,0:T(8,128)}), f32[64,512]{1,0:T(8,128)}) %reduce-scatter.21.cloned.1.call-update) | async-done | bytes 131088 | tf_op jit(solution)/shard_map/reduce_scatter | solution.py:204
  735.3 106.9 %reduce-scatter.23.cloned.1.call-done = f32[64,2048]{1,0:T(8,128)} async-done(((f32[1024,2048]{1,0:T(8,128)}), f32[64,2048]{1,0:T(8,128)}) %reduce-scatter.23.cloned.1.call-update) | async-done | bytes 524304 | tf_op jit(solution)/shard_map/reduce_scatter | solution.py:205
  842.3 107.6 %reduce-scatter.25.cloned.1.call-done = f32[64,2048]{1,0:T(8,128)} async-done(((f32[1024,2048]{1,0:T(8,128)}), f32[64,2048]{1,0:T(8,128)}) %reduce-scatter.25.cloned.1.call-update) | async-done | bytes 524304 | tf_op jit(solution)/shard_map/reduce_scatter | solution.py:206
  949.9 89.0 %reduce-scatter.19.cloned.1.call-done = f32[64,3,512]{2,0,1:T(8,128)} async-done(((f32[1024,3,512]{2,0,1:T(8,128)}), f32[64,3,512]{2,0,1:T(8,128)}) %reduce-scatter.19.cloned.1.call-update) | async-done | bytes 393232 | tf_op jit(solution)/shard_map/reduce_scatter | solution.py:203
  (137 shorter events, 28.7 us)
Async XLA Ops:
  7.2 51.3 %all-gather.9.cloned.1.call-start = ((), (), s32[]{:S(2)}) async-start(), calls=%async_computation.8 | async-start | bytes 3342336 | tf_op jit(solution)/shard_map/all_gather | solution.py:108
  7.9 92.9 %all-gather.13.cloned.1.call-start = ((), (), s32[]{:S(2)}) async-start(), calls=%async_computation.10 | async-start | bytes 1310720 | tf_op jit(solution)/shard_map/all_gather | solution.py:137
  61.6 4.2 copy-start.17
  63.7 1.2 copy-start.2
  65.8 61.6 %all-gather.11.cloned.1.call-start = ((), (), s32[]{:S(2)}) async-start(), calls=%async_computation.9 | async-start | bytes 1310720 | tf_op jit(solution)/shard_map/all_gather | solution.py:138
  99.2 66.5 %all-gather.15.cloned.1.call-start = ((), (), s32[]{:S(2)}) async-start(), calls=%async_computation.11 | async-start | bytes 1114112 | tf_op jit(solution)/shard_map/all_gather | solution.py:109
  99.8 161.4 %all-reduce.8.cloned.1.call-start = ((), (), s32[]{:S(2)}) async-start(), calls=%async_computation.12 | async-start | bytes 2097152 | tf_op jit(solution)/shard_map/psum | solution.py:144
  100.8 2.9 copy-start.5
  103.7 3.2 copy-start
  106.9 62.8 %copy-start.18 = (bf16[4,64]{1,0:T(4,128)(2,1)S(1)}, bf16[4,64]{1,0:T(4,128)(2,1)}, u32[]{:S(2)}) copy-start(bf16[4,64]{1,0:T(4,128)(2,1)} %param.20) | copy-start | bytes 1540
  106.9 93.5 %copy-start.19 = (bf16[2,64]{1,0:T(2,128)(2,1)S(1)}, bf16[2,64]{1,0:T(2,128)(2,1)}, u32[]{:S(2)}) copy-start(bf16[2,64]{1,0:T(2,128)(2,1)} %param.19) | copy-start | bytes 772
  106.9 122.4 %copy-start.16 = (bf16[16,8]{0,1:T(8,128)(2,1)S(1)}, bf16[16,8]{0,1:T(8,128)(2,1)}, u32[]{:S(2)}) copy-start(bf16[16,8]{0,1:T(8,128)(2,1)} %param.18) | copy-start | bytes 772
  132.9 128.3 %copy-start.8 = (bf16[8,64,256]{2,1,0:T(8,128)(2,1)}, bf16[8,64,256]{2,1,0:T(8,128)(2,1)S(1)}, u32[]{:S(2)}) copy-start(bf16[8,64,256]{2,1,0:T(8,128)(2,1)S(1)} %convolution_convert_fusion.1) | copy-start | bytes 786436
  132.9 128.3 %copy-start.3 = (bf16[1,256,1024]{2,1,0:T(8,128)(2,1)S(1)}, bf16[1,256,1024]{2,1,0:T(8,128)(2,1)}, u32[]{:S(2)}) copy-start(bf16[1,256,1024]{2,1,0:T(8,128)(2,1)} %param.11) | copy-start | bytes 1572868
  168.3 94.6 %all-gather.17.cloned.1.call-start = ((), (), s32[]{:S(2)}) async-start(), calls=%async_computation.13 | async-start | bytes 4456448 | tf_op jit(solution)/shard_map/all_gather | solution.py:110
  168.9 142.7 %all-gather.19.cloned.1.call-start = ((), (), s32[]{:S(2)}) async-start(), calls=%async_computation.14 | async-start | bytes 4456448 | tf_op jit(solution)/shard_map/all_gather | solution.py:111
  169.7 185.2 %all-reduce.10.cloned.1.call-start = ((), (), s32[]{:S(2)}) async-start(), calls=%async_computation.15 | async-start | bytes 2097152 | tf_op jit(solution)/shard_map/psum | solution.py:151
  266.5 45.1 %copy-start.10 = (f32[256,2048]{1,0:T(8,128)}, f32[256,2048]{1,0:T(8,128)S(1)}, u32[]{:S(2)}) copy-start(f32[256,2048]{1,0:T(8,128)S(1)} %convolution_add_fusion) | copy-start | bytes 6291460
  316.0 40.9 %copy-start.7 = (bf16[1,256,1024]{2,1,0:T(8,128)(2,1)S(1)}, bf16[1,256,1024]{2,1,0:T(8,128)(2,1)}, u32[]{:S(2)}) copy-start(bf16[1,256,1024]{2,1,0:T(8,128)(2,1)} %param.21) | copy-start | bytes 1572868
  316.1 88.4 %all-reduce.12.cloned.1.call-start = ((), (), s32[]{:S(2)}) async-start(), calls=%async_computation.16 | async-start | bytes 2097152 | tf_op jit(solution)/shard_map/psum | solution.py:165
  354.9 4.9 copy-start.11
  354.9 4.9 copy-start.21
  359.8 2.2 copy-start.20
  361.8 2.4 copy-start.12
  364.3 100.5 %reduce-scatter.15.cloned.1.call-start = ((), (), s32[]{:S(2)}) async-start(), calls=%async_computation.17 | async-start | bytes 2621440 | tf_op jit(solution)/shard_map/reduce_scatter | solution.py:178
  411.1 7.6 copy-start.6
  416.7 2.0 copy-start.1
  420.9 88.9 %reduce-scatter.17.cloned.1.call-start = ((), (), s32[]{:S(2)}) async-start(), calls=%async_computation.18 | async-start | bytes 2621440 | tf_op jit(solution)/shard_map/reduce_scatter | solution.py:179
  427.6 141.1 %reduce-scatter.27.cloned.1.call-start = ((), (), s32[]{:S(2)}) async-start(), calls=%async_computation.24 | async-start | bytes 557056
  429.9 197.6 %reduce-scatter.29.cloned.1.call-start = ((), (), s32[]{:S(2)}) async-start(), calls=%async_computation.25 | async-start | bytes 557056
  435.8 253.8 %all-reduce.14.cloned.1.call-start = ((), (), s32[]{:S(2)}) async-start(), calls=%async_computation.19 | async-start | bytes 2097152 | tf_op jit(solution)/shard_map/psum | solution.py:190
  466.6 51.5 %copy-start.9 = (bf16[8,64,256]{2,1,0:T(8,128)(2,1)S(1)}, bf16[8,64,256]{2,1,0:T(8,128)(2,1)}, u32[]{:S(2)}) copy-start(bf16[8,64,256]{2,1,0:T(8,128)(2,1)} %copy-done.8) | copy-start | bytes 786436
  517.9 217.5 %reduce-scatter.21.cloned.1.call-start = ((), (), s32[]{:S(2)}) async-start(), calls=%async_computation.21 | async-start | bytes 2228224 | tf_op jit(solution)/shard_map/reduce_scatter | solution.py:204
  520.0 322.3 %reduce-scatter.23.cloned.1.call-start = ((), (), s32[]{:S(2)}) async-start(), calls=%async_computation.22 | async-start | bytes 8912896 | tf_op jit(solution)/shard_map/reduce_scatter | solution.py:205
  526.0 423.9 %reduce-scatter.25.cloned.1.call-start = ((), (), s32[]{:S(2)}) async-start(), calls=%async_computation.23 | async-start | bytes 8912896 | tf_op jit(solution)/shard_map/reduce_scatter | solution.py:206
  532.2 0.9 copy-start.13
  532.2 1.0 copy-start.14
  532.2 1.1 copy-start.15
  532.2 3.5 copy-start.4
  532.2 506.7 %reduce-scatter.19.cloned.1.call-start = ((), (), s32[]{:S(2)}) async-start(), calls=%async_computation.20 | async-start | bytes 6684672 | tf_op jit(solution)/shard_map/reduce_scatter | solution.py:203
  545.8 0.7 copy-start.22
Sparse Core Ops, SparseCore 0:
  10.2 48.1 all-gather.8
  65.9 28.7 all-gather.12
  99.3 28.0 all-gather.10
  129.4 36.1 all-gather.14
  168.5 39.0 all-reduce.7
  209.6 50.7 all-gather.16
  262.6 48.9 all-gather.18
  316.2 38.6 all-reduce.9
  364.4 40.0 all-reduce.11
  421.1 43.6 reduce-scatter.14
  467.0 42.8 reduce-scatter.16
  513.3 55.3 reduce-scatter.26
  572.3 55.1 reduce-scatter.28
  630.2 39.1 all-reduce.13
  673.5 61.7 reduce-scatter.20
  739.8 102.3 reduce-scatter.22
  846.7 103.0 reduce-scatter.24
  954.2 84.6 reduce-scatter.18
where the time goes:
time: 1050 us
  waiting for transfers between devices  728 us (69%)
  blocking collectives  181 us (17%)
  matrix products  67.8 us (6%)
  local copies, waits for them, and re-layouts  31.7 us (3%)
  other arithmetic  20.3 us (2%)
  between operations  16 us (2%)
    reduce_scatter x1, waiting for transfers between devices, on_device(): lax.psum_scatter(down_part, ('dp', 'ctx'), scatter_dimension=0, tiled=True)  108 us
    reduce_scatter x1, waiting for transfers between devices, on_device(): lax.psum_scatter(up_part, ('dp', 'ctx'), scatter_dimension=0, tiled=True)  107 us
    reduce_scatter x1, waiting for transfers between devices, on_device(): lax.psum_scatter(qkv_part, ('dp', 'ctx'), scatter_dimension=0, tiled=True)  89 us
    unnamed x20, waiting for transfers between devices  81 us
    unnamed x1, blocking collectives  59.2 us
    all_gather x1, waiting for transfers between devices, on_device(): lax.all_gather(qkv_weight, ('dp', 'ctx'), axis=0, tiled=True)  50.5 us
    all_gather x1, waiting for transfers between devices, on_device(): lax.all_gather(down_weight, ('dp', 'ctx'), axis=0, tiled=True)  45.1 us
    reduce_scatter x1, waiting for transfers between devices, on_device(): lax.psum_scatter(out_part, ('dp', 'ctx'), scatter_dimension=0, tiled=True)  43.4 us
  transfers between devices with their start and end apart: 18, of which 14 were waited for; matrix products, arithmetic and copies ran while one was open for 7% of the time, Pallas kernels for 0%

commit v1 on v0

v1 whole, which is shorter than its diff:
```python
import functools
import math

import jax
import jax.numpy as jnp
from jax import lax
from jax.experimental import pallas as pl
from jax.experimental.pallas import tpu as pltpu
from jax.sharding import PartitionSpec as P

EPSILON = 1e-05
SCALE = 0.125
NEG_BIG = -1000000000.0
INV_ROOT_TWO = 1.0 / math.sqrt(2.0)
INV_ROOT_TWO_PI = 1.0 / math.sqrt(2.0 * math.pi)


def contract_last(left, right):
    return lax.dot_general(
        left, right, (((1,), (1,)), ((), ())), preferred_element_type=jnp.float32
    )


def contract_first(left, right):
    return lax.dot_general(
        left, right, (((0,), (0,)), ((), ())), preferred_element_type=jnp.float32
    )


def layer_norm(hidden_in, gain, shift):
    centred = hidden_in - jnp.mean(hidden_in, axis=-1, keepdims=True)
    variance = jnp.mean(centred * centred, axis=-1, keepdims=True)
    inv_std = lax.rsqrt(variance + EPSILON)
    normed = centred * inv_std
    return (normed * gain + shift, normed, inv_std)


def norm_back(grad_out, normed, inv_std, gain):
    grad_normed = grad_out * gain
    first_mean = jnp.mean(grad_normed, axis=-1, keepdims=True)
    second_mean = jnp.mean(grad_normed * normed, axis=-1, keepdims=True)
    grad_in = inv_std * (grad_normed - first_mean - normed * second_mean)
    return (grad_in, jnp.sum(grad_out * normed, axis=0), jnp.sum(grad_out, axis=0))


def gelu_parts(pre_act):
    cdf_val = 0.5 * (1.0 + jax.scipy.special.erf(pre_act * INV_ROOT_TWO))
    return (
        pre_act * cdf_val,
        cdf_val + pre_act * jnp.exp(-0.5 * pre_act * pre_act) * INV_ROOT_TWO_PI,
    )


def block_scores(queries, key_rows, valid):
    scores = (
        jnp.einsum("qhd,khd->hqk", queries, key_rows, preferred_element_type=jnp.float32) * SCALE
    )
    return jnp.where(valid[None, None, :], scores, NEG_BIG)


def attend_forward(inputs):
    queries, key_rows, value_rows, valid = inputs
    scores = block_scores(queries, key_rows, valid)
    peak = jnp.max(scores, axis=-1, keepdims=True)
    log_total = peak + jnp.log(jnp.sum(jnp.exp(scores - peak), axis=-1, keepdims=True))
    probs = jnp.exp(scores - log_total).astype(jnp.bfloat16)
    mixed = jnp.einsum(
        "hqk,khd->qhd", probs, value_rows, preferred_element_type=jnp.float32
    ).astype(jnp.bfloat16)
    return (mixed, log_total)


def attend_backward(inputs):
    queries, key_rows, value_rows, valid, mixed, log_total, grad_mixed = inputs
    scores = block_scores(queries, key_rows, valid)
    probs = jnp.exp(scores - log_total)
    grad_values = jnp.einsum(
        "hqk,qhd->khd", probs.astype(jnp.bfloat16), grad_mixed, preferred_element_type=jnp.float32
    )
    grad_probs = jnp.einsum(
        "qhd,khd->hqk", grad_mixed, value_rows, preferred_element_type=jnp.float32
    )
    inner = jnp.einsum("qhd,qhd->hq", grad_mixed.astype(jnp.float32), mixed.astype(jnp.float32))
    grad_scores = (probs * (grad_probs - inner[:, :, None])).astype(jnp.bfloat16)
    grad_queries = (
        jnp.einsum("hqk,khd->qhd", grad_scores, key_rows, preferred_element_type=jnp.float32)
        * SCALE
    )
    grad_keys = (
        jnp.einsum("hqk,qhd->khd", grad_scores, queries, preferred_element_type=jnp.float32) * SCALE
    )
    return (grad_queries, grad_keys, grad_values)


def comm_kernel(sizes, kinds, copies, *refs):
    n_outer, n_core, n_ctx, n_tensor = sizes
    count = len(kinds)
    ins, outs = refs[:count], refs[count : 2 * count]
    send_sem, recv_sem, own_sem = refs[2 * count :]
    dp, ctx, tensor = (lax.axis_index(name) for name in ("dp", "ctx", "tensor"))
    outer, core = dp // n_core, dp % n_core

    def coords(offset, sign=1):
        def move(at, step, size):
            return at if step == 0 else (at + (step if sign > 0 else size - step)) % size

        outer_at = move(outer, offset[0], n_outer)
        core_at = move(core, offset[1], n_core)
        return outer_at * n_core + core_at, move(ctx, offset[2], n_ctx), move(tensor, offset[3], n_tensor)

    def device(offset):
        dp_at, ctx_at, tensor_at = coords(offset)
        return {"dp": dp_at, "ctx": ctx_at, "tensor": tensor_at}

    offsets = peer_offsets(sizes, kinds)
    barrier = pltpu.get_barrier_semaphore()
    for offset in offsets:
        pl.semaphore_signal(
            barrier, inc=1, device_id=device(offset), device_id_type=pl.DeviceIdType.MESH
        )
    pl.semaphore_wait(barrier, len(offsets))

    started, used = [], [0]

    def put(source, target, offset):
        number = used[0]
        used[0] += 1
        copy = pltpu.make_async_remote_copy(
            src_ref=source,
            dst_ref=target,
            send_sem=send_sem.at[number],
            recv_sem=recv_sem.at[number],
            device_id=device(offset),
            device_id_type=pl.DeviceIdType.MESH,
        )
        copy.start()
        started.append(copy)
        return number

    def arrived(number, target, offset):
        pltpu.make_async_remote_copy(
            src_ref=target,
            dst_ref=target,
            send_sem=send_sem.at[number],
            recv_sem=recv_sem.at[number],
            device_id=device(offset),
            device_id_type=pl.DeviceIdType.MESH,
        ).wait_recv()

    partner = (0, 1, 0, 0)
    pending, own_copies = [], []
    first = {}
    for at, kind in enumerate(kinds):
        source, target = ins[at], outs[at]
        index = functools.partial(slot_of, kind, n_ctx)
        mine = index(*coords((0, 0, 0, 0)))
        if kind == "swap":
            for offset in direct_offsets(sizes, kind):
                number = put(source, target.at[offset[3] - 1], offset)
                pending.append((number, target.at[offset[3] - 1], offset))
            continue
        if kind in ("ctx", "dp", "all"):
            for offset in direct_offsets(sizes, kind):
                number = put(source.at[index(*coords(offset))], target.at[mine], offset)
                pending.append((number, target.at[index(*coords(offset, -1))], offset))
            own = pltpu.make_async_copy(source.at[mine], target.at[mine], own_sem.at[at])
        else:
            stage = []
            if kind == "wg":
                for step in range(1, n_ctx):
                    offset = (0, 0, step, 0)
                    stage.append((put(source, target.at[mine], offset), offset))
            crossing = []
            for step in range(1, n_outer):
                offset = (step, 0, 0, 0)
                crossing.append((put(source, target.at[mine], offset), offset, (0, 0, 0, 0)))
            pending.append(
                (put(source, target.at[mine], partner), target.at[index(*coords(partner, -1))], partner)
            )
            own = pltpu.make_async_copy(source, target.at[mine], own_sem.at[at])
            first[at] = (stage, crossing)
        own.start()
        own_copies.append(own)
    for at in first:
        target = outs[at]
        index = functools.partial(slot_of, kinds[at], n_ctx)
        stage, crossing = first[at]
        for number, offset in stage:
            slot = index(*coords(offset, -1))
            arrived(number, target.at[slot], offset)
            for step in range(1, n_outer):
                across = (step, 0, 0, 0)
                crossing.append((put(target.at[slot], target.at[slot], across), across, offset))
            both = (0, 1, offset[2], 0)
            pending.append(
                (put(target.at[slot], target.at[slot], partner), target.at[index(*coords(both, -1))], partner)
            )
    for at in first:
        target = outs[at]
        index = functools.partial(slot_of, kinds[at], n_ctx)
        for number, across, offset in first[at][1]:
            origin = (across[0], 0, offset[2], 0)
            slot = index(*coords(origin, -1))
            arrived(number, target.at[slot], across)
            both = (across[0], 1, offset[2], 0)
            pending.append(
                (put(target.at[slot], target.at[slot], partner), target.at[index(*coords(both, -1))], partner)
            )
    for number, target, offset in pending:
        arrived(number, target, offset)
    for own in own_copies:
        own.wait()
    for copy in started:
        copy.wait_send()


def slot_of(kind, n_ctx, dp_at, ctx_at, tensor_at):
    if kind == "ctx":
        return ctx_at
    if kind in ("dp", "dpg"):
        return dp_at
    return dp_at * n_ctx + ctx_at


def direct_offsets(sizes, kind):
    n_outer, n_core, n_ctx, n_tensor = sizes
    if kind == "swap":
        return [(0, 0, 0, step) for step in range(1, n_tensor)]
    if kind == "ctx":
        return [(0, 0, step, 0) for step in range(1, n_ctx)]
    ctx_steps = range(n_ctx) if kind == "all" else range(1)
    return [
        (o, c, k, 0) for k in ctx_steps for o in range(n_outer) for c in range(n_core) if o + c + k
    ]


def peer_offsets(sizes, kinds):
    n_outer, n_core, n_ctx, n_tensor = sizes
    found = set()
    for kind in kinds:
        if kind in ("wg", "dpg"):
            found.update((o, 0, 0, 0) for o in range(1, n_outer))
            found.add((0, 1, 0, 0))
            if kind == "wg":
                found.update((0, 0, k, 0) for k in range(1, n_ctx))
        else:
            found.update(direct_offsets(sizes, kind))
    return sorted(found)


def exchange(sizes, number, ops):
    n_outer, n_core, n_ctx, n_tensor = sizes
    n_dp = n_outer * n_core
    kinds = tuple(kind for kind, _ in ops)
    shapes, copies, moved = [], 0, 0
    for kind, array in ops:
        if kind == "swap":
            lead, sends = (n_tensor - 1,), n_tensor - 1
        elif kind == "dpg":
            lead, sends = (n_dp,), n_dp - 1
        elif kind == "wg":
            lead, sends = (n_dp * n_ctx,), n_dp * n_ctx - 1
        else:
            lead, sends = (), array.shape[0] - 1
        shapes.append(jax.ShapeDtypeStruct(lead + array.shape, array.dtype))
        copies += sends
        moved += math.prod(lead + array.shape) * array.dtype.itemsize
    vmem = pl.BlockSpec(memory_space=pltpu.VMEM)
    return pl.pallas_call(
        functools.partial(comm_kernel, sizes, kinds, copies),
        out_shape=tuple(shapes),
        in_specs=[vmem] * len(ops),
        out_specs=tuple(
            pl.BlockSpec(memory_space=pl.ANY) if kind == "wg" else vmem for kind in kinds
        ),
        scratch_shapes=[
            pltpu.SemaphoreType.DMA((copies,)),
            pltpu.SemaphoreType.DMA((copies,)),
            pltpu.SemaphoreType.DMA((len(ops),)),
        ],
        compiler_params=pltpu.CompilerParams(
            collective_id=number, has_side_effects=True, vmem_limit_bytes=60 * 2**20
        ),
        cost_estimate=pl.CostEstimate(
            flops=0, bytes_accessed=moved * 10, transcendentals=0
        ),
        name=f"exchange_{number}",
    )(*(array for _, array in ops))


def pack(parts, lead, unit):
    flat = jnp.concatenate([part.reshape(lead, -1) for part in parts], axis=1)
    wide = -(-flat.shape[1] // unit) * unit
    return jnp.pad(flat, ((0, 0), (0, wide - flat.shape[1]))).reshape(lead, wide // 128, 128)


def unpack(packed, shapes):
    flat = packed.reshape(packed.shape[0], -1)
    out, at = [], 0
    for shape in shapes:
        size = math.prod(shape)
        out.append(flat[:, at : at + size].reshape((packed.shape[0],) + shape))
        at += size
    return out


def on_device(
    sizes,
    tokens,
    seq_lengths,
    qkv_weight,
    out_weight,
    up_weight,
    down_weight,
    head_bias,
    hidden_bias,
    norm_gains,
    out_biases,
    cotangent,
):
    n_outer, n_core, n_ctx, n_tensor = sizes
    n_dp = n_outer * n_core
    shards = n_dp * n_ctx
    seq_count, local_len, width = tokens.shape
    row_count = seq_count * local_len
    total_len = n_ctx * local_len
    local_width = qkv_weight.shape[2]
    feature_rows = width // n_dp
    token_rows = tokens.reshape(row_count, width)

    def feature_slices(rows):
        return rows.reshape(row_count, n_dp, feature_rows).transpose(1, 0, 2)

    smalls = (head_bias, hidden_bias, norm_gains, out_biases)
    qkv_got, out_got, up_got, down_got, small_got, token_slices = exchange(
        sizes,
        1,
        [
            ("wg", qkv_weight.reshape(qkv_weight.shape[0], 3 * local_width)),
            ("wg", out_weight),
            ("wg", up_weight),
            ("wg", down_weight),
            ("wg", pack(smalls, 1, 2048)[0]),
            ("dp", feature_slices(token_rows)),
        ],
    )
    qkv_full = qkv_got.reshape(width, 3 * local_width)
    out_full = out_got.reshape(width, -1)
    up_full = up_got.reshape(width, -1)
    down_full = down_got.reshape(width, -1)
    head_full, hidden_full, gains_full, biases_full = (
        part.transpose(1, 0, 2).reshape(part.shape[1], -1)
        for part in unpack(small_got, [small.shape for small in smalls])
    )
    local_heads = head_full.shape[0]
    head_size = head_full.shape[1] // 2
    heads_here = local_heads // n_ctx
    group_width = heads_here * head_size
    bias_query = head_full[:, :head_size].reshape(local_width).astype(jnp.float32)
    bias_value = head_full[:, head_size:].reshape(local_width).astype(jnp.float32)
    bias_hidden = hidden_full.reshape(-1).astype(jnp.float32)
    gains_wide = gains_full.astype(jnp.float32)
    biases_wide = biases_full.astype(jnp.float32)

    def to_positions(chunks, parts):
        return (
            chunks.reshape(n_ctx, parts, seq_count, local_len, group_width)
            .transpose(1, 2, 0, 3, 4)
            .reshape(parts, seq_count, total_len, heads_here, head_size)
        )

    def by_position(parts):
        return (
            jnp.stack(parts)
            .reshape(len(parts), seq_count, n_ctx, local_len, group_width)
            .transpose(2, 0, 1, 3, 4)
            .reshape(n_ctx, len(parts), row_count, group_width)
        )

    def by_heads(rows, parts):
        return rows.reshape(row_count, parts, n_ctx, group_width).transpose(2, 1, 0, 3)

    def to_rows(chunks, parts):
        return (
            chunks.reshape(n_ctx, parts, row_count, group_width)
            .transpose(2, 1, 0, 3)
            .reshape(row_count, parts * local_width)
        )

    projected = jnp.dot(token_rows, qkv_full, preferred_element_type=jnp.float32)
    shift = jnp.concatenate([bias_query, jnp.zeros_like(bias_query), bias_value])
    projected = (projected + shift).astype(jnp.bfloat16)
    (qkv_chunks,) = exchange(sizes, 2, [("ctx", by_heads(projected, 3))])
    queries, key_rows, value_rows = to_positions(qkv_chunks, 3)
    valid = jnp.arange(total_len)[None, :] < seq_lengths[:, None]
    mixed, log_total = lax.map(attend_forward, (queries, key_rows, value_rows, valid))
    (mixed_chunks,) = exchange(sizes, 3, [("ctx", by_position([mixed]))])
    attn_flat = to_rows(mixed_chunks, 1)
    attn_part = contract_last(attn_flat, out_full)
    attn_other, attn_all = exchange(sizes, 4, [("swap", attn_part), ("dpg", attn_flat)])
    attn_proj = attn_part + jnp.sum(attn_other, axis=0)
    first_sum = token_rows.astype(jnp.float32) + attn_proj + biases_wide[0]
    normed_one, z_one, rstd_one = layer_norm(first_sum, gains_wide[0], biases_wide[1])
    normed_low = normed_one.astype(jnp.bfloat16)
    pre_act = jnp.dot(normed_low, up_full, preferred_element_type=jnp.float32) + bias_hidden
    activated, slope = gelu_parts(pre_act)
    hidden_low = activated.astype(jnp.bfloat16)
    mlp_part = contract_last(hidden_low, down_full)
    mlp_other, hidden_all, normed_slices = exchange(
        sizes,
        5,
        [("swap", mlp_part), ("dpg", hidden_low), ("dp", feature_slices(normed_low))],
    )
    mlp_out = mlp_part + jnp.sum(mlp_other, axis=0)
    second_sum = normed_one + mlp_out + biases_wide[2]
    result, z_two, rstd_two = layer_norm(second_sum, gains_wide[1], biases_wide[3])
    output = result.astype(jnp.bfloat16).reshape(seq_count, local_len, width)
    grad_out = cotangent.reshape(row_count, width).astype(jnp.float32)
    grad_two, gain_two_grad, shift_two_grad = norm_back(grad_out, z_two, rstd_two, gains_wide[1])
    grad_two_low = grad_two.astype(jnp.bfloat16)
    grad_hidden = jnp.dot(grad_two_low, down_full, preferred_element_type=jnp.float32)
    grad_pre = grad_hidden * slope
    grad_pre_low = grad_pre.astype(jnp.bfloat16)
    hidden_part = jnp.sum(grad_pre, axis=0).reshape(hidden_full.shape)
    normed_part = contract_last(grad_pre_low, up_full)
    normed_other, grad_pre_all, grad_two_slices = exchange(
        sizes,
        6,
        [("swap", normed_part), ("dpg", grad_pre_low), ("dp", feature_slices(grad_two_low))],
    )

    def over_rows(slices, wide):
        return contract_first(
            slices.reshape(n_dp * row_count, feature_rows), wide.reshape(n_dp * row_count, -1)
        )

    down_grad = lax.psum_scatter(
        over_rows(grad_two_slices, hidden_all), "ctx", scatter_dimension=0, tiled=True
    )
    up_grad = lax.psum_scatter(
        over_rows(normed_slices, grad_pre_all), "ctx", scatter_dimension=0, tiled=True
    )
    grad_normed = normed_part + jnp.sum(normed_other, axis=0) + grad_two
    grad_one, gain_one_grad, shift_one_grad = norm_back(grad_normed, z_one, rstd_one, gains_wide[0])
    grad_one_low = grad_one.astype(jnp.bfloat16)
    grad_attn = jnp.dot(grad_one_low, out_full, preferred_element_type=jnp.float32).astype(
        jnp.bfloat16
    )
    grad_chunks, grad_one_slices = exchange(
        sizes, 7, [("ctx", by_heads(grad_attn, 1)), ("dp", feature_slices(grad_one_low))]
    )
    grad_mixed = to_positions(grad_chunks, 1)[0]
    out_grad = over_rows(grad_one_slices, attn_all)
    grad_queries, grad_keys, grad_values = lax.map(
        attend_backward, (queries, key_rows, value_rows, valid, mixed, log_total, grad_mixed)
    )
    (proj_chunks,) = exchange(
        sizes,
        8,
        [
            (
                "ctx",
                by_position(
                    [part.astype(jnp.bfloat16) for part in (grad_queries, grad_keys, grad_values)]
                ),
            )
        ],
    )
    grad_proj = to_rows(proj_chunks, 3)
    input_part = contract_last(grad_proj, qkv_full)
    head_rows = jnp.concatenate(
        [jnp.sum(grad_queries, axis=(0, 1)), jnp.sum(grad_values, axis=(0, 1))], axis=1
    )
    head_part = lax.dynamic_update_slice(
        jnp.zeros((local_heads, 2 * head_size), jnp.float32),
        head_rows,
        (lax.axis_index("ctx") * heads_here, 0),
    )
    gains_part = jnp.stack([gain_one_grad, gain_two_grad])
    biases_part = jnp.stack(
        [jnp.sum(grad_one, axis=0), shift_one_grad, jnp.sum(grad_two, axis=0), shift_two_grad]
    )
    small_parts = [
        part.reshape(part.shape[0], shards, -1).transpose(1, 0, 2)
        for part in (head_part, hidden_part, gains_part, biases_part)
    ]
    input_other, proj_all, small_sums, out_blocks = exchange(
        sizes,
        9,
        [
            ("swap", input_part),
            ("dpg", grad_proj),
            ("all", pack(small_parts, shards, 1024)),
            ("ctx", out_grad.reshape(n_ctx, feature_rows // n_ctx, -1)),
        ],
    )
    input_grad = (input_part + jnp.sum(input_other, axis=0) + grad_one).reshape(
        seq_count, local_len, width
    )
    qkv_part = over_rows(token_slices, proj_all)
    (qkv_blocks,) = exchange(
        sizes, 10, [("ctx", qkv_part.reshape(n_ctx, feature_rows // n_ctx, -1))]
    )
    qkv_grad = jnp.sum(qkv_blocks, axis=0).reshape(-1, 3, local_width)
    small_grads = unpack(
        jnp.sum(small_sums, axis=0)[None], [part.shape[1:] for part in small_parts]
    )
    return (
        output,
        input_grad,
        qkv_grad,
        jnp.sum(out_blocks, axis=0),
        up_grad,
        down_grad,
        *(part[0] for part in small_grads),
    )


def solution(mesh):
    in_specs = (
        P("dp", "ctx", None),
        P("dp"),
        P(("dp", "ctx"), None, "tensor"),
        P(("dp", "ctx"), "tensor"),
        P(("dp", "ctx"), "tensor"),
        P(("dp", "ctx"), "tensor"),
        P("tensor", ("dp", "ctx")),
        P("tensor", ("dp", "ctx")),
        P(None, ("dp", "ctx")),
        P(None, ("dp", "ctx")),
        P("dp", "ctx", None),
    )
    out_specs = (
        P("dp", "ctx", None),
        P("dp", "ctx", None),
        P(("dp", "ctx"), None, "tensor"),
        P(("dp", "ctx"), "tensor"),
        P(("dp", "ctx"), "tensor"),
        P(("dp", "ctx"), "tensor"),
        P("tensor", ("dp", "ctx")),
        P("tensor", ("dp", "ctx")),
        P(None, ("dp", "ctx")),
        P(None, ("dp", "ctx")),
    )
    n_core = 2 if mesh.shape["dp"] % 2 == 0 else 1
    sizes = (mesh.shape["dp"] // n_core, n_core, mesh.shape["ctx"], mesh.shape["tensor"])
    return jax.shard_map(
        functools.partial(on_device, sizes), mesh=mesh, in_specs=in_specs, out_specs=out_specs, check_vma=False
    )
```

time: 1050 us -> 486 us (0.46)
  waiting for transfers between devices: 728 us -> 0.04 us
  Pallas kernels: 0 us -> 353 us
  blocking collectives: 181 us -> 0 us
  matrix products: 67.8 us -> 51.7 us
    reduce_scatter x6 -> x2, waiting for transfers between devices: 419 us -> 0.01 us  [the longest x1 0.01 us: on_device(): lax.psum_scatter(over_rows(normed_slices, grad_pre_all), 'ctx', scatter_d...]
    pallas_call x0 -> x10, Pallas kernels: none -> 353 us  [exchange(): pl.pallas_call(functools.partial(comm_kernel, sizes, kinds, copies), out_...]
    all_gather x6 -> x0, waiting for transfers between devices: 149 us -> none  [the longest x1 50.5 us: on_device(): lax.all_gather(qkv_weight, ('dp', 'ctx'), axis=0, tiled=True)]
    all_gather x4 -> x0, blocking collectives: 122 us -> none  [the longest x1 31.7 us: on_device(): lax.all_gather(hidden_bias, ('dp', 'ctx'), axis=1, tiled=True)]
    unnamed x20 -> x2, waiting for transfers between devices: 81 us -> 0.03 us
    psum x4 -> x0, waiting for transfers between devices: 78.8 us -> none  [the longest x1 40.2 us: on_device(): lax.psum(contract_last(grad_pre_low, up_back), 'tensor') + grad_two]
    unnamed x1 -> x0, blocking collectives: 59.2 us -> none
  transfers between devices with their start and end apart: 18 -> 2, of which waited for: 14 -> 0; matrix products, arithmetic and copies ran while one was open for 7% -> 11% of each run, Pallas kernels for 0% -> 26%
where the time goes in v1:
time: 486 us; the launch traced here: 480 us
  Pallas kernels  353 us (73%)
  matrix products  51.7 us (11%)
  local copies, waits for them, and re-layouts  37.6 us (8%)
  other arithmetic  22.6 us (5%)
  between operations  15.4 us (3%)
    pallas_call x10, Pallas kernels, exchange(): pl.pallas_call(functools.partial(comm_kernel, sizes, kinds, copies), out_...  353 us
    dot_general x4, matrix products, contract_first(): lax.dot_general(left, right, (((0,), (0,)), ((), ())), preferred_element_...  16.3 us
    unnamed x58, local copies, waits for them, and re-layouts  11 us
    dot_general x4, matrix products, contract_last(): lax.dot_general(left, right, (((1,), (1,)), ((), ())), preferred_element_...  9.84 us
  transfers between devices with their start and end apart: 2, of which 0 were waited for; matrix products, arithmetic and copies ran while one was open for 11% of the time, Pallas kernels for 26%

profile of v1, /device:TPU:0, one launch (start us, length us, event | category | flops | bytes accessed | tf_op | source)
XLA Modules:
  0.0 480.3 jit_solution(15466751482945110275)
XLA Ops:
  7.2 1.7 copy.109
  12.0 1.2 copy.52
  13.3 1.0 copy.53
  15.0 92.3 %exchange_1.1 = (bf16[16,64,1536]{2,1,0:T(8,128)(2,1)}, bf16[16,64,512]{2,1,0:T(8,128)(2,1)}, bf16[16,64,2048]{2,1,0:T(8,128)(2,1)}, bf16[16,64,2048]{2,1,0:T(8,...) custom-call(bf16[64,1536]{1,0:T(8,128)(2,1)} %bitcast.244, bf16[64,512]{1,0:T(8,128)(2,1)} %refs_1_.1, ...), custom_call_target="tpu_custom_call" | custom-call | bytes 131727360 | tf_op jit(solution)/shard_map/exchange_1/pallas_call | solution.py:269
  109.6 3.0 fusion.2
  112.6 1.2 copy.56
  113.8 23.8 %exchange_2.1 = bf16[4,3,256,128]{3,2,1,0:T(8,128)(2,1)} custom-call(bf16[4,3,256,128]{3,2,1,0:T(8,128)(2,1)} %bitcast.225), custom_call_target="tpu_custom_call" | custom-call | bytes 7864320 | tf_op jit(solution)/shard_map/exchange_2/pallas_call | solution.py:269
  137.5 1.2 fusion.42
  140.5 1.6 fusion.1
  142.1 2.3 exponential_reduce_fusion
  145.3 2.3 fusion
  147.7 2.0 copy-done.1
  151.6 13.8 %exchange_3.1 = bf16[4,1,256,128]{3,2,1,0:T(8,128)(2,1)} custom-call(bf16[4,1,256,128]{3,2,1,0:T(8,128)(2,1)} %copy.61.refs_0_), custom_call_target="tpu_custom_call" | custom-call | bytes 2621440 | tf_op jit(solution)/shard_map/exchange_3/pallas_call | solution.py:269
  165.3 1.2 copy.62
  167.2 1.4 fusion.32.refs_0_
  168.8 28.0 %exchange_4.1 = (f32[1,256,1024]{2,1,0:T(8,128)}, bf16[4,256,512]{2,1,0:T(8,128)(2,1)}) custom-call(f32[256,1024]{1,0:T(8,128)} %fusion.32.refs_0_, bf16[256,512]{1,0:T(8,128)(2,1)} %bitcast.239), custom_call_target="tpu_custom_call" | custom-call | bytes 20971520 | tf_op jit(solution)/shard_map/exchange_4/pallas_call | solution.py:269
  196.8 1.9 fusion.39
  200.2 3.0 multiply_convert_fusion.1
  203.1 1.0 copy-done.18
  204.1 2.3 fusion.46.refs_0_
  206.4 34.9 %exchange_5.1 = (f32[1,256,1024]{2,1,0:T(8,128)}, bf16[4,256,2048]{2,1,0:T(8,128)(2,1)}, bf16[4,256,256]{2,1,0:T(8,128)(2,1)}) custom-call(f32[256,1024]{1,0:T(8,128)} %fusion.46.refs_0_, bf16[256,2048]{1,0:T(8,128)(2,1)} %copy-done.18, bf16[4,256,256]{2,1,0:T(8,128)(2,1)} %bitcast.230), custom_call_target="tpu_custom_call" | custom-call | bytes 57671680 | tf_op jit(solution)/shard_map/exchange_5/pallas_call | solution.py:269
  241.3 2.0 fusion.37
  244.2 2.4 fusion.34
  246.8 3.4 fusion.41
  250.2 2.3 fusion.47.refs_0_
  253.3 34.8 %exchange_6.1 = (f32[1,256,1024]{2,1,0:T(8,128)}, bf16[4,256,2048]{2,1,0:T(8,128)(2,1)}, bf16[4,256,256]{2,1,0:T(8,128)(2,1)}) custom-call(f32[256,1024]{1,0:T(8,128)} %fusion.47.refs_0_, bf16[256,2048]{1,0:T(8,128)(2,1)} %copy-done.17, bf16[4,256,256]{2,1,0:T(8,128)(2,1)} %bitcast.232), custom_call_target="tpu_custom_call" | custom-call | bytes 57671680 | tf_op jit(solution)/shard_map/exchange_6/pallas_call | solution.py:269
  288.1 4.8 %convolution_bitcast_fusion.1 = f32[256,2048]{1,0:T(8,128)} fusion(bf16[4,256,256]{2,1,0:T(8,128)(2,1)S(1)} %copy-done.20, bf16[4,256,2048]{2,1,0:T(8,128)(2,1)} %get-tuple-element.100), kind=kOutput, calls=%fused_computation.10 | convolution fusion | flops 1073741824 | bytes 6815744 | tf_op jit(solution)/shard_map/dot_general | solution.py:25
  292.9 5.0 %convolution_bitcast_fusion = f32[256,2048]{1,0:T(8,128)} fusion(bf16[4,256,256]{2,1,0:T(8,128)(2,1)} %get-tuple-element.101, bf16[4,256,2048]{2,1,0:T(8,128)(2,1)} %get-tuple-element.102), kind=kOutput, calls=%fused_computation.9 | convolution fusion | flops 1073741824 | bytes 6815744 | tf_op jit(solution)/shard_map/dot_general | solution.py:25
  298.0 2.0 multiply_reduce_fusion
  302.7 15.5 %exchange_7.1 = (bf16[4,1,256,128]{3,2,1,0:T(8,128)(2,1)}, bf16[4,256,256]{2,1,0:T(8,128)(2,1)}) custom-call(bf16[4,1,256,128]{3,2,1,0:T(8,128)(2,1)} %bitcast.240, bf16[4,256,256]{2,1,0:T(8,128)(2,1)} %bitcast.235), custom_call_target="tpu_custom_call" | custom-call | bytes 7864320 | tf_op jit(solution)/shard_map/exchange_7/pallas_call | solution.py:269
  318.2 1.1 copy.70
  319.5 3.7 fusion.44
  323.7 5.2 %multiply_convert_fusion = bf16[2,1024,1024]{1,2,0:T(8,128)(2,1)S(1)} fusion(f32[2,1024,1024]{1,2,0:T(8,128)} %copy-done, f32[2,1024]{1,0:T(2,128)S(1)} %fusion.28, f32[2,1024]{1,0:T(2,128)S(1)} %log_add_fusion, pred[1024]{0:T(1024)(128)(4,1)S(1)} %iota_compare_fusion.1, bf16[1024,2,64]{0,2,1:T(8,128)(2,1)S(1)} %squeeze.36, bf16[1024,2,64]{0,2,1:T(8,128)(2,1)S(1)} %copy-done.13), kind=kOutput, calls=%fused_computation | convolution fusion | flops 281018368 | bytes 13124608 | tf_op jit(solution)/shard_map/while/body/eval_jaxpr/qhd,khd->hqk/dot_general | solution.py:80
  329.0 1.9 copy-done.2
  330.9 1.4 fusion.14
  332.7 3.1 fusion.43
  337.2 32.7 %exchange_8.1 = bf16[4,3,256,128]{3,2,1,0:T(8,128)(2,1)} custom-call(bf16[4,3,256,128]{3,2,1,0:T(8,128)(2,1)} %maximum_bitcast_fusion.refs_0_), custom_call_target="tpu_custom_call" | custom-call | bytes 7864320 | tf_op jit(solution)/shard_map/exchange_8/pallas_call | solution.py:269
  369.9 1.7 copy.78
  374.1 1.2 copy.83
  375.4 1.2 copy.84
  376.6 2.5 fusion.49.refs_3_
  379.1 3.9 fusion.48.refs_0_
  383.0 45.2 %exchange_9.1 = (f32[1,256,1024]{2,1,0:T(8,128)}, bf16[4,256,1536]{2,1,0:T(8,128)(2,1)}, f32[16,8,128]{2,1,0:T(8,128)}, f32[4,64,512]{2,1,0:T(8,128)}) custom-call(f32[256,1024]{1,0:T(8,128)} %fusion.48.refs_0_, bf16[256,1536]{1,0:T(8,128)(2,1)} %copy-done.11, f32[16,8,128]{2,1,0:T(8,128)} %bitcast.250, f32[4,64,512]{2,1,0:T(8,128)} %fusion.49.refs_3_), custom_call_target="tpu_custom_call" | custom-call | bytes 47841280 | tf_op jit(solution)/shard_map/exchange_9/pallas_call | solution.py:269
  428.2 4.0 fusion.50.refs_0_
  432.2 32.1 %exchange_10.1 = f32[4,64,1536]{2,1,0:T(8,128)} custom-call(f32[4,64,1536]{2,1,0:T(8,128)} %fusion.50.refs_0_), custom_call_target="tpu_custom_call" | custom-call | bytes 15728640 | tf_op jit(solution)/shard_map/exchange_10/pallas_call | solution.py:269
  464.3 1.5 reduce_sum.236
  466.7 1.7 reduce_sum.237
  472.2 1.2 fusion.20
  (158 shorter events, 26.4 us)
Async XLA Ops:
  7.2 102.4 %copy-start.16 = (bf16[1,256,1024]{2,1,0:T(8,128)(2,1)S(1)}, bf16[1,256,1024]{2,1,0:T(8,128)(2,1)}, u32[]{:S(2)}) copy-start(bf16[1,256,1024]{2,1,0:T(8,128)(2,1)} %param.11) | copy-start | bytes 1572868
  7.2 466.2 %reduce-scatter.3.cloned.1.call-start = ((), (), s32[]{:S(2)}) async-start(), calls=%async_computation.2 | async-start | bytes 2621440 | tf_op jit(solution)/shard_map/reduce_scatter | solution.py:440
  139.1 8.6 %copy-start.12 = (bf16[1024,2,64]{0,2,1:T(8,128)(2,1)}, bf16[1024,2,64]{0,2,1:T(8,128)(2,1)S(1)}, u32[]{:S(2)}) copy-start(bf16[1024,2,64]{0,2,1:T(8,128)(2,1)S(1)} %squeeze.33) | copy-start | bytes 786436
  140.1 2.0 copy-start.14
  140.5 1.6 copy-start.9
  142.1 3.2 copy-start
  147.6 2.0 copy-start.1
  149.6 17.6 %copy-start.6 = (bf16[16,64,512]{2,1,0:T(8,128)(2,1)S(1)}, bf16[16,64,512]{2,1,0:T(8,128)(2,1)}, u32[]{:S(2)}) copy-start(bf16[16,64,512]{2,1,0:T(8,128)(2,1)} %get-tuple-element.86) | copy-start | bytes 3145732
  196.8 3.3 copy-start.21
  200.2 4.0 copy-start.23
  203.1 1.0 copy-start.18
  206.4 37.2 %copy-start.3 = (bf16[1,256,1024]{2,1,0:T(8,128)(2,1)S(1)}, bf16[1,256,1024]{2,1,0:T(8,128)(2,1)}, u32[]{:S(2)}) copy-start(bf16[1,256,1024]{2,1,0:T(8,128)(2,1)} %param.21) | copy-start | bytes 1572868
  244.2 2.5 copy-start.24
  246.7 3.4 copy-start.22
  250.2 3.1 copy-start.17
  250.2 37.9 %copy-start.20 = (bf16[4,256,256]{2,1,0:T(8,128)(2,1)S(1)}, bf16[4,256,256]{2,1,0:T(8,128)(2,1)}, u32[]{:S(2)}) copy-start(bf16[4,256,256]{2,1,0:T(8,128)(2,1)} %get-tuple-element.99) | copy-start | bytes 1572868
  292.9 180.5 %reduce-scatter.5.cloned.1.call-start = ((), (), s32[]{:S(2)}) async-start(), calls=%async_computation.3 | async-start | bytes 2621440 | tf_op jit(solution)/shard_map/reduce_scatter | solution.py:437
  292.9 5.0 %copy-start.5 = (f32[256,1024]{1,0:T(8,128)S(1)}, f32[256,1024]{1,0:T(8,128)}, u32[]{:S(2)}) copy-start(f32[256,1024]{1,0:T(8,128)} %fusion.47.refs_0_) | copy-start | bytes 3145732
  298.0 2.5 copy-start.7
  302.7 21.0 %copy-start.13 = (bf16[1024,2,64]{0,2,1:T(8,128)(2,1)S(1)}, bf16[1024,2,64]{0,2,1:T(8,128)(2,1)}, u32[]{:S(2)}) copy-start(bf16[1024,2,64]{0,2,1:T(8,128)(2,1)} %copy-done.12) | copy-start | bytes 786436
  323.7 7.2 %copy-start.15 = (bf16[1024,2,64]{0,2,1:T(8,128)(2,1)S(1)}, bf16[1024,2,64]{0,2,1:T(8,128)(2,1)}, u32[]{:S(2)}) copy-start(bf16[1024,2,64]{0,2,1:T(8,128)(2,1)} %copy-done.14) | copy-start | bytes 786436
  329.0 1.9 copy-start.2
  330.9 1.8 copy-start.10
  335.8 36.1 %copy-start.4 = (bf16[1,256,1024]{2,1,0:T(8,128)(2,1)S(1)}, bf16[1,256,1024]{2,1,0:T(8,128)(2,1)}, u32[]{:S(2)}) copy-start(bf16[1,256,1024]{2,1,0:T(8,128)(2,1)} %param.21) | copy-start | bytes 1572868
  372.0 11.0 %copy-start.11 = (bf16[256,1536]{1,0:T(8,128)(2,1)}, bf16[256,1536]{1,0:T(8,128)(2,1)S(1)}, u32[]{:S(2)}) copy-start(bf16[256,1536]{1,0:T(8,128)(2,1)S(1)} %reshape.305.refs_1_) | copy-start | bytes 2359300
  432.2 40.0 %copy-start.8 = (f32[256,1024]{1,0:T(8,128)S(1)}, f32[256,1024]{1,0:T(8,128)}, u32[]{:S(2)}) copy-start(f32[256,1024]{1,0:T(8,128)} %fusion.48.refs_0_) | copy-start | bytes 3145732
  432.2 40.0 %copy-start.19 = (f32[1,256,1024]{2,1,0:T(8,128)S(1)}, f32[1,256,1024]{2,1,0:T(8,128)}, u32[]{:S(2)}) copy-start(f32[1,256,1024]{2,1,0:T(8,128)} %get-tuple-element.95) | copy-start | bytes 3145732
Sparse Core Ops, SparseCore 0:
  293.0 48.0 reduce-scatter.2
  344.0 50.9 reduce-scatter.4

commit v2 on v1

--- a/solution.py
+++ b/solution.py
@@ -159,11 +159,13 @@
                 number = put(source, target.at[offset[3] - 1], offset)
                 pending.append((number, target.at[offset[3] - 1], offset))
             continue
-        if kind in ("ctx", "dp", "all"):
+        if kind in ("ctx", "cg", "dp", "all"):
             for offset in direct_offsets(sizes, kind):
-                number = put(source.at[index(*coords(offset))], target.at[mine], offset)
+                block = source if kind == "cg" else source.at[index(*coords(offset))]
+                number = put(block, target.at[mine], offset)
                 pending.append((number, target.at[index(*coords(offset, -1))], offset))
-            own = pltpu.make_async_copy(source.at[mine], target.at[mine], own_sem.at[at])
+            block = source if kind == "cg" else source.at[mine]
+            own = pltpu.make_async_copy(block, target.at[mine], own_sem.at[at])
         else:
             stage = []
             if kind == "wg":
@@ -215,7 +217,7 @@
 
 
 def slot_of(kind, n_ctx, dp_at, ctx_at, tensor_at):
-    if kind == "ctx":
+    if kind in ("ctx", "cg"):
         return ctx_at
     if kind in ("dp", "dpg"):
         return dp_at
@@ -226,7 +228,7 @@
     n_outer, n_core, n_ctx, n_tensor = sizes
     if kind == "swap":
         return [(0, 0, 0, step) for step in range(1, n_tensor)]
-    if kind == "ctx":
+    if kind in ("ctx", "cg"):
         return [(0, 0, step, 0) for step in range(1, n_ctx)]
     ctx_steps = range(n_ctx) if kind == "all" else range(1)
     return [
@@ -258,6 +260,8 @@
             lead, sends = (n_tensor - 1,), n_tensor - 1
         elif kind == "dpg":
             lead, sends = (n_dp,), n_dp - 1
+        elif kind == "cg":
+            lead, sends = (n_ctx,), n_ctx - 1
         elif kind == "wg":
             lead, sends = (n_dp * n_ctx,), n_dp * n_ctx - 1
         else:
@@ -332,22 +336,20 @@
         return rows.reshape(row_count, n_dp, feature_rows).transpose(1, 0, 2)
 
     smalls = (head_bias, hidden_bias, norm_gains, out_biases)
-    qkv_got, out_got, up_got, down_got, small_got, token_slices = exchange(
+    qkv_got, out_got, small_got, token_slices = exchange(
         sizes,
         1,
         [
             ("wg", qkv_weight.reshape(qkv_weight.shape[0], 3 * local_width)),
             ("wg", out_weight),
-            ("wg", up_weight),
-            ("wg", down_weight),
             ("wg", pack(smalls, 1, 2048)[0]),
             ("dp", feature_slices(token_rows)),
         ],
     )
     qkv_full = qkv_got.reshape(width, 3 * local_width)
     out_full = out_got.reshape(width, -1)
-    up_full = up_got.reshape(width, -1)
-    down_full = down_got.reshape(width, -1)
+    up_full = lax.all_gather(up_weight, ("dp", "ctx"), axis=0, tiled=True)
+    down_full = lax.all_gather(down_weight, ("dp", "ctx"), axis=0, tiled=True)
     head_full, hidden_full, gains_full, biases_full = (
         part.transpose(1, 0, 2).reshape(part.shape[1], -1)
         for part in unpack(small_got, [small.shape for small in smalls])
@@ -406,10 +408,11 @@
     activated, slope = gelu_parts(pre_act)
     hidden_low = activated.astype(jnp.bfloat16)
     mlp_part = contract_last(hidden_low, down_full)
-    mlp_other, hidden_all, normed_slices = exchange(
+    half = n_dp // 2
+    mlp_other, hidden_all, token_low = exchange(
         sizes,
         5,
-        [("swap", mlp_part), ("dpg", hidden_low), ("dp", feature_slices(normed_low))],
+        [("swap", mlp_part), ("dpg", hidden_low), ("cg", token_slices[:half])],
     )
     mlp_out = mlp_part + jnp.sum(mlp_other, axis=0)
     second_sum = normed_one + mlp_out + biases_wide[2]
@@ -423,10 +426,15 @@
     grad_pre_low = grad_pre.astype(jnp.bfloat16)
     hidden_part = jnp.sum(grad_pre, axis=0).reshape(hidden_full.shape)
     normed_part = contract_last(grad_pre_low, up_full)
-    normed_other, grad_pre_all, grad_two_slices = exchange(
+    normed_other, grad_pre_all, grad_two_slices, token_high = exchange(
         sizes,
         6,
-        [("swap", normed_part), ("dpg", grad_pre_low), ("dp", feature_slices(grad_two_low))],
+        [
+            ("swap", normed_part),
+            ("dpg", grad_pre_low),
+            ("dp", feature_slices(grad_two_low)),
+            ("cg", token_slices[half:]),
+        ],
     )
 
     def over_rows(slices, wide):
@@ -436,9 +444,6 @@
 
     down_grad = lax.psum_scatter(
         over_rows(grad_two_slices, hidden_all), "ctx", scatter_dimension=0, tiled=True
-    )
-    up_grad = lax.psum_scatter(
-        over_rows(normed_slices, grad_pre_all), "ctx", scatter_dimension=0, tiled=True
     )
     grad_normed = normed_part + jnp.sum(normed_other, axis=0) + grad_two
     grad_one, gain_one_grad, shift_one_grad = norm_back(grad_normed, z_one, rstd_one, gains_wide[0])
@@ -446,26 +451,34 @@
     grad_attn = jnp.dot(grad_one_low, out_full, preferred_element_type=jnp.float32).astype(
         jnp.bfloat16
     )
-    grad_chunks, grad_one_slices = exchange(
-        sizes, 7, [("ctx", by_heads(grad_attn, 1)), ("dp", feature_slices(grad_one_low))]
+    grad_chunks, grad_one_slices, normed_slices = exchange(
+        sizes,
+        7,
+        [
+            ("ctx", by_heads(grad_attn, 1)),
+            ("dp", feature_slices(grad_one_low)),
+            ("dp", feature_slices(normed_low)),
+        ],
+    )
+    up_grad = lax.psum_scatter(
+        over_rows(normed_slices, grad_pre_all), "ctx", scatter_dimension=0, tiled=True
     )
     grad_mixed = to_positions(grad_chunks, 1)[0]
     out_grad = over_rows(grad_one_slices, attn_all)
     grad_queries, grad_keys, grad_values = lax.map(
         attend_backward, (queries, key_rows, value_rows, valid, mixed, log_total, grad_mixed)
     )
-    (proj_chunks,) = exchange(
-        sizes,
-        8,
-        [
-            (
-                "ctx",
-                by_position(
-                    [part.astype(jnp.bfloat16) for part in (grad_queries, grad_keys, grad_values)]
-                ),
-            )
-        ],
-    )
+    proj_parts = by_position(
+        [part.astype(jnp.bfloat16) for part in (grad_queries, grad_keys, grad_values)]
+    )
+    proj_wide = proj_parts.transpose(0, 2, 1, 3).reshape(n_ctx * row_count, 3 * group_width)
+    proj_chunks, proj_all = exchange(sizes, 8, [("ctx", proj_parts), ("dpg", proj_wide)])
+    token_all = (
+        jnp.concatenate([token_low, token_high], axis=1)
+        .transpose(1, 0, 2, 3)
+        .reshape(n_dp * n_ctx * row_count, feature_rows)
+    )
+    qkv_part = contract_first(token_all, proj_all.reshape(n_dp * n_ctx * row_count, -1))
     grad_proj = to_rows(proj_chunks, 3)
     input_part = contract_last(grad_proj, qkv_full)
     head_rows = jnp.concatenate(
@@ -484,24 +497,24 @@
         part.reshape(part.shape[0], shards, -1).transpose(1, 0, 2)
         for part in (head_part, hidden_part, gains_part, biases_part)
     ]
-    input_other, proj_all, small_sums, out_blocks = exchange(
+    input_other, small_sums, out_blocks, qkv_blocks = exchange(
         sizes,
         9,
         [
             ("swap", input_part),
-            ("dpg", grad_proj),
             ("all", pack(small_parts, shards, 1024)),
             ("ctx", out_grad.reshape(n_ctx, feature_rows // n_ctx, -1)),
+            ("ctx", qkv_part.reshape(n_ctx, feature_rows // n_ctx, -1)),
         ],
     )
     input_grad = (input_part + jnp.sum(input_other, axis=0) + grad_one).reshape(
         seq_count, local_len, width
     )
-    qkv_part = over_rows(token_slices, proj_all)
-    (qkv_blocks,) = exchange(
-        sizes, 10, [("ctx", qkv_part.reshape(n_ctx, feature_rows // n_ctx, -1))]
-    )
-    qkv_grad = jnp.sum(qkv_blocks, axis=0).reshape(-1, 3, local_width)
+    qkv_grad = (
+        qkv_blocks.reshape(n_ctx, -1, 3, group_width)
+        .transpose(1, 2, 0, 3)
+        .reshape(-1, 3, local_width)
+    )
     small_grads = unpack(
         jnp.sum(small_sums, axis=0)[None], [part.shape[1:] for part in small_parts]
     )

time: 486 us -> 439 us (0.903)
  Pallas kernels: 353 us -> 302 us
  local copies, waits for them, and re-layouts: 37.6 us -> 43.6 us
    pallas_call x10 -> x9, Pallas kernels: 353 us -> 302 us  [exchange(): pl.pallas_call(functools.partial(comm_kernel, sizes, kinds, copies), out_...]
    unnamed x58 -> x53, local copies, waits for them, and re-layouts: 11 us -> 12.1 us
  transfers between devices with their start and end apart: 2 -> 4, of which waited for: 0 -> 0; matrix products, arithmetic and copies ran while one was open for 11% -> 20% of each run, Pallas kernels for 26% -> 49%
where the time goes in v2:
time: 439 us; the launch traced here: 438 us
  Pallas kernels  302 us (69%)
  matrix products  53.9 us (12%)
  local copies, waits for them, and re-layouts  43.6 us (10%)
  other arithmetic  21.4 us (5%)
  between operations  15 us (3%)
    pallas_call x9, Pallas kernels, exchange(): pl.pallas_call(functools.partial(comm_kernel, sizes, kinds, copies), out_...  302 us
    dot_general x4, matrix products, contract_first(): lax.dot_general(left, right, (((0,), (0,)), ((), ())), preferred_element_...  14.6 us
    dot_general x4, matrix products, contract_last(): lax.dot_general(left, right, (((1,), (1,)), ((), ())), preferred_element_...  12.7 us
    unnamed x53, local copies, waits for them, and re-layouts  12.1 us
  transfers between devices with their start and end apart: 4, of which 0 were waited for; matrix products, arithmetic and copies ran while one was open for 20% of the time, Pallas kernels for 49%

profile of v2, /device:TPU:0, one launch (start us, length us, event | category | flops | bytes accessed | tf_op | source)
XLA Modules:
  0.0 437.6 jit_solution(3574106418740047027)
XLA Ops:
  8.7 1.6 copy.154
  13.5 1.2 copy.93
  14.7 1.0 copy.94
  16.4 49.1 %exchange_1.1 = (bf16[16,64,1536]{2,1,0:T(8,128)(2,1)}, bf16[16,64,512]{2,1,0:T(8,128)(2,1)}, bf16[16,16,128]{2,1,0:T(8,128)(2,1)}, bf16[4,256,256]{2,1,0:T(8,128)(2,1)}) custom-call(bf16[64,1536]{1,0:T(8,128)(2,1)} %bitcast.256, bf16[64,512]{1,0:T(8,128)(2,1)} %refs_1_.1, bf16[16,128]{1,0:T(8,128)(2,1)} %bitcast.271, bf16[4,256,256]{2,1,0:T(8,128)(2,1)} %bitcast.243), custom_call_target="tpu_custom_call" | custom-call | bytes 47841280 | tf_op jit(solution)/shard_map/exchange_1/pallas_call | solution.py:273
  67.9 3.0 fusion.2
  70.9 1.2 copy.97
  72.1 40.1 %exchange_2.1 = bf16[4,3,256,128]{3,2,1,0:T(8,128)(2,1)} custom-call(bf16[4,3,256,128]{3,2,1,0:T(8,128)(2,1)} %bitcast.235), custom_call_target="tpu_custom_call" | custom-call | bytes 7864320 | tf_op jit(solution)/shard_map/exchange_2/pallas_call | solution.py:273
  112.2 1.2 fusion.44
  115.1 1.6 fusion.1
  116.7 2.3 exponential_reduce_fusion
  119.9 2.3 fusion
  122.2 2.0 copy-done.1
  126.1 18.8 %exchange_3.1 = bf16[4,1,256,128]{3,2,1,0:T(8,128)(2,1)} custom-call(bf16[4,1,256,128]{3,2,1,0:T(8,128)(2,1)} %copy.102.refs_0_), custom_call_target="tpu_custom_call" | custom-call | bytes 2621440 | tf_op jit(solution)/shard_map/exchange_3/pallas_call | solution.py:273
  145.0 1.2 copy.103
  147.2 1.4 fusion.34.refs_0_
  148.6 28.1 %exchange_4.1 = (f32[1,256,1024]{2,1,0:T(8,128)}, bf16[4,256,512]{2,1,0:T(8,128)(2,1)}) custom-call(f32[256,1024]{1,0:T(8,128)} %fusion.34.refs_0_, bf16[256,512]{1,0:T(8,128)(2,1)} %bitcast.248), custom_call_target="tpu_custom_call" | custom-call | bytes 20971520 | tf_op jit(solution)/shard_map/exchange_4/pallas_call | solution.py:273
  176.7 1.8 fusion.41
  180.7 5.1 %multiply_convert_fusion.1 = (bf16[256,2048]{1,0:T(8,128)(2,1)S(1)}, f32[256,2048]{1,0:T(8,128)}) fusion(f32[2048]{0:T(1024)S(1)} %reshape.320, bf16[256,1024]{1,0:T(8,128)(2,1)S(1)} %fusion.26, bf16[1024,2048]{1,0:T(8,128)(2,1)} %all-gather.3.cloned.1.call-done), kind=kOutput, calls=%fused_computation.18 | convolution fusion | flops 1076887552 | bytes 7872512 | tf_op jit(solution)/shard_map/dot_general | solution.py:407
  185.8 4.8 %fusion.49.refs_0_ = f32[256,1024]{1,0:T(8,128)} fusion(bf16[256,2048]{1,0:T(8,128)(2,1)S(1)} %get-tuple-element.182.refs_1_, bf16[1024,2048]{1,0:T(8,128)(2,1)} %all-gather.5.cloned.1.call-done), kind=kOutput, calls=%fused_computation.124 | convolution fusion | flops 1073741824 | bytes 6291456 | tf_op jit(solution)/shard_map/dot_general | solution.py:19
  190.6 36.2 %exchange_5.1 = (f32[1,256,1024]{2,1,0:T(8,128)}, bf16[4,256,2048]{2,1,0:T(8,128)(2,1)}, bf16[4,2,256,256]{3,2,1,0:T(8,128)(2,1)}) custom-call(f32[256,1024]{1,0:T(8,128)} %fusion.49.refs_0_, bf16[256,2048]{1,0:T(8,128)(2,1)} %copy-done.11, bf16[2,256,256]{2,1,0:T(8,128)(2,1)} %get-tuple-element.175.refs_2_), custom_call_target="tpu_custom_call" | custom-call | bytes 62914560 | tf_op jit(solution)/shard_map/exchange_5/pallas_call | solution.py:273
  226.8 2.0 fusion.39
  229.6 1.3 fusion.36
  231.8 2.0 fusion.43
  233.9 1.0 copy-done.14
  234.9 2.3 fusion.50.refs_0_
  237.2 35.5 %exchange_6.1 = (f32[1,256,1024]{2,1,0:T(8,128)}, bf16[4,256,2048]{2,1,0:T(8,128)(2,1)}, bf16[4,256,256]{2,1,0:T(8,128)(2,1)}, bf16[4,2,256,256]{3,2,1,0:T(8,128)(2,1)}) custom-call(f32[256,1024]{1,0:T(8,128)} %fusion.50.refs_0_, bf16[256,2048]{1,0:T(8,128)(2,1)} %copy-done.14, bf16[4,256,256]{2,1,0:T(8,128)(2,1)} %bitcast.246, ...), custom_call_target="tpu_custom_call" | custom-call | bytes 68157440 | tf_op jit(solution)/shard_map/exchange_6/pallas_call | solution.py:273
  272.7 2.2 multiply_reduce_fusion
  277.7 17.8 %exchange_7.1 = (bf16[4,1,256,128]{3,2,1,0:T(8,128)(2,1)}, bf16[4,256,256]{2,1,0:T(8,128)(2,1)}, bf16[4,256,256]{2,1,0:T(8,128)(2,1)}) custom-call(bf16[4,1,256,128]{3,2,1,0:T(8,128)(2,1)} %bitcast.249, bf16[4,256,256]{2,1,0:T(8,128)(2,1)} %bitcast.244, bf16[4,256,256]{2,1,0:T(8,128)(2,1)} %bitcast.241), custom_call_target="tpu_custom_call" | custom-call | bytes 13107200 | tf_op jit(solution)/shard_map/exchange_7/pallas_call | solution.py:273
  295.5 5.0 %convolution_bitcast_fusion.1 = f32[256,2048]{1,0:T(8,128)} fusion(bf16[4,256,256]{2,1,0:T(8,128)(2,1)} %get-tuple-element.103, bf16[4,256,2048]{2,1,0:T(8,128)(2,1)} %get-tuple-element.104), kind=kOutput, calls=%fused_computation.10 | convolution fusion | flops 1073741824 | bytes 6815744 | tf_op jit(solution)/shard_map/dot_general | solution.py:25
  301.2 4.8 %convolution_bitcast_fusion = f32[256,2048]{1,0:T(8,128)} fusion(bf16[4,256,256]{2,1,0:T(8,128)(2,1)S(1)} %copy-done.16, bf16[4,256,2048]{2,1,0:T(8,128)(2,1)} %get-tuple-element.106), kind=kOutput, calls=%fused_computation.9 | convolution fusion | flops 1073741824 | bytes 6815744 | tf_op jit(solution)/shard_map/dot_general | solution.py:25
  305.9 3.7 fusion.46
  310.2 5.4 %multiply_convert_fusion = bf16[2,1024,1024]{1,2,0:T(8,128)(2,1)S(1)} fusion(f32[2,1024,1024]{1,2,0:T(8,128)} %copy-done, f32[2,1024]{1,0:T(2,128)S(1)} %fusion.28, f32[2,1024]{1,0:T(2,128)S(1)} %log_add_fusion, pred[1024]{0:T(1024)(128)(4,1)S(1)} %iota_compare_fusion.1, bf16[1024,2,64]{0,2,1:T(8,128)(2,1)S(1)} %squeeze.36, bf16[1024,2,64]{0,2,1:T(8,128)(2,1)S(1)} %copy-done.8), kind=kOutput, calls=%fused_computation | convolution fusion | flops 281018368 | bytes 13124608 | tf_op jit(solution)/shard_map/while/body/eval_jaxpr/qhd,khd->hqk/dot_general | solution.py:80
  315.6 1.9 copy-done.2
  317.5 1.4 fusion.14
  319.3 3.1 fusion.45
  322.9 1.0 fusion.30
  324.6 1.1 copy.166
  325.6 29.5 %exchange_8.1 = (bf16[4,3,256,128]{3,2,1,0:T(8,128)(2,1)}, bf16[4,1024,384]{2,1,0:T(8,128)(2,1)}) custom-call(bf16[4,3,256,128]{3,2,1,0:T(8,128)(2,1)} %get-tuple-element.166.refs_0_, bf16[1024,384]{1,0:T(8,128)(2,1)} %bitcast.233), custom_call_target="tpu_custom_call" | custom-call | bytes 39321600 | tf_op jit(solution)/shard_map/exchange_8/pallas_call | solution.py:273
  355.2 2.3 copy.121
  359.5 2.0 copy.126
  361.8 2.9 copy.128
  364.7 2.8 fusion.52.refs_2_
  367.5 4.1 fusion.51.refs_0_
  371.6 2.0 fusion.53.refs_3_
  373.7 47.1 %exchange_9.1 = (f32[1,256,1024]{2,1,0:T(8,128)}, f32[16,8,128]{2,1,0:T(8,128)}, f32[4,64,512]{2,1,0:T(8,128)}, f32[4,64,384]{2,1,0:T(8,128)}) custom-call(f32[256,1024]{1,0:T(8,128)} %fusion.51.refs_0_, f32[16,8,128]{2,1,0:T(8,128)} %bitcast.259, f32[4,64,512]{2,1,0:T(8,128)} %fusion.52.refs_2_, f32[4,64,384]{2,1,0:T(8,128)} %fusion.53.refs_3_), custom_call_target="tpu_custom_call" | custom-call | bytes 20316160 | tf_op jit(solution)/shard_map/exchange_9/pallas_call | solution.py:273
  420.8 1.1 reshape.316
  423.1 1.7 reduce_sum.227
  428.6 2.5 fusion.20
  (162 shorter events, 29.0 us)
Async XLA Ops:
  7.2 60.7 %copy-start.9 = (bf16[1,256,1024]{2,1,0:T(8,128)(2,1)S(1)}, bf16[1,256,1024]{2,1,0:T(8,128)(2,1)}, u32[]{:S(2)}) copy-start(bf16[1,256,1024]{2,1,0:T(8,128)(2,1)} %param.11) | copy-start | bytes 1572868
  7.2 173.5 %all-gather.3.cloned.1.call-start = ((), (), s32[]{:S(2)}) async-start(), calls=%async_computation.2 | async-start | bytes 4456448 | tf_op jit(solution)/shard_map/all_gather | solution.py:351
  7.9 177.8 %all-gather.5.cloned.1.call-start = ((), (), s32[]{:S(2)}) async-start(), calls=%async_computation.3 | async-start | bytes 4456448 | tf_op jit(solution)/shard_map/all_gather | solution.py:352
  8.7 422.4 %reduce-scatter.3.cloned.1.call-start = ((), (), s32[]{:S(2)}) async-start(), calls=%async_computation.4 | async-start | bytes 2621440 | tf_op jit(solution)/shard_map/reduce_scatter | solution.py:463
  113.7 8.5 %copy-start.7 = (bf16[1024,2,64]{0,2,1:T(8,128)(2,1)}, bf16[1024,2,64]{0,2,1:T(8,128)(2,1)S(1)}, u32[]{:S(2)}) copy-start(bf16[1024,2,64]{0,2,1:T(8,128)(2,1)S(1)} %squeeze.33) | copy-start | bytes 786436
  116.7 3.2 copy-start
  122.2 2.0 copy-start.1
  124.2 23.0 %copy-start.4 = (bf16[16,64,512]{2,1,0:T(8,128)(2,1)S(1)}, bf16[16,64,512]{2,1,0:T(8,128)(2,1)}, u32[]{:S(2)}) copy-start(bf16[16,64,512]{2,1,0:T(8,128)(2,1)} %get-tuple-element.88) | copy-start | bytes 3145732
  148.6 31.2 %copy-start.15 = (bf16[4,256,256]{2,1,0:T(8,128)(2,1)S(1)}, bf16[4,256,256]{2,1,0:T(8,128)(2,1)}, u32[]{:S(2)}) copy-start(bf16[4,256,256]{2,1,0:T(8,128)(2,1)} %get-tuple-element.90) | copy-start | bytes 1572868
  185.8 4.8 %copy-start.11 = (bf16[256,2048]{1,0:T(8,128)(2,1)}, bf16[256,2048]{1,0:T(8,128)(2,1)S(1)}, u32[]{:S(2)}) copy-start(bf16[256,2048]{1,0:T(8,128)(2,1)S(1)} %get-tuple-element.182.refs_1_) | copy-start | bytes 3145732
  190.6 38.5 %copy-start.3 = (bf16[1,256,1024]{2,1,0:T(8,128)(2,1)S(1)}, bf16[1,256,1024]{2,1,0:T(8,128)(2,1)}, u32[]{:S(2)}) copy-start(bf16[1,256,1024]{2,1,0:T(8,128)(2,1)} %param.21) | copy-start | bytes 1572868
  228.8 3.0 copy-start.19
  228.8 3.0 copy-start.21
  231.8 3.1 copy-start.18
  233.9 1.0 copy-start.14
  272.7 2.7 copy-start.5
  295.5 5.3 %copy-start.17 = (bf16[4,1,256,128]{3,2,1,0:T(8,128)(2,1)S(1)}, bf16[4,1,256,128]{3,2,1,0:T(8,128)(2,1)}, u32[]{:S(2)}) copy-start(bf16[4,1,256,128]{3,2,1,0:T(8,128)(2,1)} %get-tuple-element.93) | copy-start | bytes 786436
  295.5 5.7 %copy-start.16 = (bf16[4,256,256]{2,1,0:T(8,128)(2,1)S(1)}, bf16[4,256,256]{2,1,0:T(8,128)(2,1)}, u32[]{:S(2)}) copy-start(bf16[4,256,256]{2,1,0:T(8,128)(2,1)} %get-tuple-element.105) | copy-start | bytes 1572868
  300.5 130.6 %reduce-scatter.5.cloned.1.call-start = ((), (), s32[]{:S(2)}) async-start(), calls=%async_computation.5 | async-start | bytes 2621440 | tf_op jit(solution)/shard_map/reduce_scatter | solution.py:445
  305.9 4.3 copy-start.8
  315.6 1.9 copy-start.2
  323.9 37.6 %copy-start.12 = (bf16[4,2,256,256]{3,2,1,0:T(8,128)(2,1)S(1)}, bf16[4,2,256,256]{3,2,1,0:T(8,128)(2,1)}, u32[]{:S(2)}) copy-start(bf16[4,2,256,256]{3,2,1,0:T(8,128)(2,1)} %get-tuple-element.97) | copy-start | bytes 3145732
  323.9 37.6 %copy-start.13 = (bf16[4,2,256,256]{3,2,1,0:T(8,128)(2,1)S(1)}, bf16[4,2,256,256]{3,2,1,0:T(8,128)(2,1)}, u32[]{:S(2)}) copy-start(bf16[4,2,256,256]{3,2,1,0:T(8,128)(2,1)} %get-tuple-element.98) | copy-start | bytes 3145732
  364.7 6.9 %copy-start.10 = (bf16[256,4096]{1,0:T(8,128)(2,1)S(1)}, bf16[256,4096]{1,0:T(8,128)(2,1)}, u32[]{:S(2)}) copy-start(bf16[256,4096]{1,0:T(8,128)(2,1)} %copy.128) | copy-start | bytes 6291460
  364.7 6.9 %copy-start.20 = (bf16[4,1024,384]{2,1,0:T(8,128)(2,1)S(1)}, bf16[4,1024,384]{2,1,0:T(8,128)(2,1)}, u32[]{:S(2)}) copy-start(bf16[4,1024,384]{2,1,0:T(8,128)(2,1)} %get-tuple-element.99) | copy-start | bytes 9437188
  373.7 55.0 %copy-start.6 = (f32[256,1024]{1,0:T(8,128)S(1)}, f32[256,1024]{1,0:T(8,128)}, u32[]{:S(2)}) copy-start(f32[256,1024]{1,0:T(8,128)} %fusion.51.refs_0_) | copy-start | bytes 3145732
Sparse Core Ops, SparseCore 0:
  10.2 73.4 all-gather.2
  85.9 65.0 all-gather.4
  300.7 52.3 reduce-scatter.2
  355.8 60.0 reduce-scatter.4
